TPU v7x, 512 devices: a whole 4x4x16 slice. The times are simulated.
512 devices in a mesh: inst: 32 (over y, z_lo, core), space: 16 (over z_hi, x).
Axes of the slice: x: 4, y: 4, z: 16 (z_hi: 4, z_lo: 4; z = z_hi * 4 + z_lo), core: 2. Of those that a mesh axis runs over, the one named last changes fastest.
Arguments:
- flow_state: float32 [32, 6, 1024, 128], P('inst', None, 'space'), may hold values from -6 to 6
- forcing: float32 [32, 6, 1024, 128], P('inst', None, 'space'), may hold values from -6 to 6
- pivot_table: float32 [8, 6, 6, 128], replicated, may hold values from -0.21 to 1, as said below
- block_offset: int32 [1024], P('space'), may hold values from 0 to 7
- line_perm: int32 [128], replicated, may hold values from 0 to 127, each once
- axial_jac: float32 [6, 6], replicated, may hold values from -2.5 to 2.5
- radial_jac: float32 [6, 6], replicated, may hold values from -2.5 to 2.5
- lower_block: float32 [6, 6], replicated, may hold values from -0.035 to 0.97, as said below
- upper_block: float32 [6, 6], replicated, may hold values from -0.035 to 0.97, as said below
Outputs:
- residual: float32 [32, 6, 1024, 128], P('inst', None, 'space')
- correction: float32 [32, 6, 1024, 128], P('inst', None, 'space')
Inputs may be any that keep to these rules, and one draw needn't show every extreme that they name: `pivot_table`: diagonal entries lie in 0.6 to 1. `lower_block`: diagonal entries lie in 0.3 to 0.97, the others in -0.035 to 0.035. `upper_block`: diagonal entries lie in 0.3 to 0.97, the others in -0.035 to 0.035.
All inputs are finite; a program needn't handle non-finite values.
Results may differ from a plain program's by a relative error of at most 0.0001.
Values sent between devices are 32-bit elements; how exact they have to be, the bound alone decides.
No kernel may reach another device: no remote copies, remote signals or barrier semaphores. Data moves between devices by JAX's collectives and lax.ppermute only.
A program may use at most 64 MiB of HBM per device.

v0:
```python
import jax
import jax.numpy as jnp
from jax import lax
from jax.experimental import pallas as pl
from jax.experimental.pallas import tpu as pltpu
from jax.sharding import PartitionSpec as P

frequency = 0.5
viscosity = 0.01
damping = 0.25

NV = 6
NQ = 8
NS = 8
NH = 2
KB = 8
LANES = 128
LEVELS = 4


def spectral_matrix(count):
    row_index = lax.broadcasted_iota(jnp.int32, (count, count), 0)
    col_index = lax.broadcasted_iota(jnp.int32, (count, count), 1)
    distance = row_index - col_index
    parity = (1 - 2 * jnp.mod(distance, 2)).astype(jnp.float32)
    phase_angle = jnp.pi * distance.astype(jnp.float32) / count
    diagonal_mask = distance == 0
    sine_value = jnp.where(diagonal_mask, 1.0, jnp.sin(phase_angle))
    first_order = jnp.where(diagonal_mask, 0.0, 0.5 * parity * jnp.cos(phase_angle) / sine_value)
    second_order = jnp.where(
        diagonal_mask, -(count * count + 2) / 12.0, -0.5 * parity / (sine_value * sine_value)
    )
    return frequency * first_order - viscosity * second_order


def shift_chunks(tile, amount):
    sub = lax.broadcasted_iota(jnp.int32, tile.shape, 0)
    lane = lax.broadcasted_iota(jnp.int32, tile.shape, 1)
    zero = jnp.zeros_like(tile)
    swapped = pltpu.roll(tile, LANES // 2, 1)
    if amount == NQ:
        return jnp.where(lane >= LANES // 2, swapped, zero)
    if amount == -NQ:
        return jnp.where(lane < LANES // 2, swapped, zero)
    near = pltpu.roll(tile, amount % NQ, 0)
    far = pltpu.roll(swapped, amount % NQ, 0)
    if amount > 0:
        return jnp.where(sub >= amount, near, jnp.where(lane >= LANES // 2, far, zero))
    return jnp.where(sub < NQ + amount, near, jnp.where(lane < LANES // 2, far, zero))


def product(left, right):
    return [
        [sum_of([left[v][x] * right[x][w] for x in range(NV)]) for w in range(NV)]
        for v in range(NV)
    ]


def sum_of(terms):
    while len(terms) > 1:
        terms = [
            terms[i] + terms[i + 1] if i + 1 < len(terms) else terms[i]
            for i in range(0, len(terms), 2)
        ]
    return terms[0]


def applied(coef_ref, index, vector):
    return [
        sum_of([coef_ref[(v * NV + w, *index)] * vector[w] for w in range(NV)]) for v in range(NV)
    ]


def tables_kernel(
    factor_ref, lower_ref, upper_ref, a_ref, b_ref, phi_ref, omega_ref, up_ref, down_ref
):
    def load(ref, t):
        return [[ref[v * NV + w, t] for w in range(NV)] for v in range(NV)]

    def keep(ref, t, value):
        for v in range(NV):
            for w in range(NV):
                ref[v * NV + w, t] = value[v][w]

    lower = [[-lower_ref[v, w] for w in range(NV)] for v in range(NV)]
    upper = [[-upper_ref[v, w] for w in range(NV)] for v in range(NV)]

    def couple(t, carry):
        factor = load(factor_ref, t)
        keep(a_ref, t, product(factor, lower))
        keep(b_ref, t, product(factor, upper))
        return carry

    lax.fori_loop(0, NS, couple, 0)
    keep(phi_ref, 0, load(a_ref, 0))
    keep(omega_ref, NS - 1, load(b_ref, NS - 1))

    def extend(t, carry):
        keep(phi_ref, t, product(load(a_ref, t), load(phi_ref, t - 1)))
        back = NS - 1 - t
        keep(omega_ref, back, product(load(b_ref, back), load(omega_ref, back + 1)))
        return carry

    lax.fori_loop(1, NS, extend, 0)
    for ref, first, sign in ((up_ref, load(phi_ref, NS - 1), 1), (down_ref, load(omega_ref, 0), -1)):
        level = first
        for step in range(LEVELS):
            keep(ref, step, level)
            if step + 1 < LEVELS:
                moved = [[shift_chunks(e, sign * 2**step) for e in row] for row in level]
                level = product(level, moved)


def time_kernel(spectral_ref, state_ref, timed_ref):
    count = spectral_ref.shape[0]
    rows = state_ref.shape[0] // count
    stacked = jnp.concatenate(
        [state_ref[pl.ds(row, count, stride=rows), :] for row in range(rows)], axis=1
    )
    result = jnp.dot(
        spectral_ref[...],
        stacked,
        precision=lax.Precision.HIGHEST,
        preferred_element_type=jnp.float32,
    )
    for row in range(rows):
        timed_ref[pl.ds(row, count, stride=rows), :] = result[:, row * LANES : (row + 1) * LANES]


def to_lines(select, value):
    parts = []
    rest = value
    for part in range(3):
        head = rest.astype(jnp.bfloat16)
        parts.append(head)
        if part < 2:
            rest = rest - head.astype(jnp.float32)
    total = None
    for head in parts:
        blank = jnp.zeros_like(head[0])
        blocks = []
        for v in range(NV):
            blocks.append(jnp.concatenate([head[v], blank], axis=1))
            blocks.append(jnp.concatenate([blank, head[v]], axis=1))
        moved = lax.dot_general(
            select,
            jnp.concatenate(blocks, axis=0),
            (((1,), (1,)), ((), ())),
            preferred_element_type=jnp.float32,
        )
        total = moved if total is None else total + moved
    return total


def local_kernel(
    state_ref, forcing_ref, low_ref, high_ref, select_ref, axial_ref, radial_ref, local_ref
):
    stations = state_ref.shape[1]
    row = lax.broadcasted_iota(jnp.int32, (stations, LANES), 0)
    state = [state_ref[v] for v in range(NV)]
    ahead = [
        jnp.where(row == stations - 1, high_ref[v : v + 1], pltpu.roll(state[v], stations - 1, 0))
        for v in range(NV)
    ]
    behind = [
        jnp.where(row == 0, low_ref[v : v + 1], pltpu.roll(state[v], 1, 0)) for v in range(NV)
    ]
    slope = [0.5 * (ahead[v] - behind[v]) for v in range(NV)]
    direct = [
        sum_of([axial_ref[v, w] * slope[w] for w in range(NV)])
        - damping * (ahead[v] + behind[v] - 4.0 * state[v])
        - forcing_ref[v]
        for v in range(NV)
    ]
    select = select_ref[...]
    lines = to_lines(select, jnp.stack(state))
    moved = to_lines(select, jnp.stack(direct))

    def tile(array, v, t):
        return array[t * NQ : (t + 1) * NQ, v * LANES : (v + 1) * LANES]

    for t in range(NS):
        outer = [
            tile(lines, v, t + 1) if t + 1 < NS else shift_chunks(tile(lines, v, 0), -1)
            for v in range(NV)
        ]
        inner = [
            tile(lines, v, t - 1) if t > 0 else shift_chunks(tile(lines, v, NS - 1), 1)
            for v in range(NV)
        ]
        slope = [0.5 * (outer[v] - inner[v]) for v in range(NV)]
        for v in range(NV):
            local_ref[v, t] = (
                sum_of([radial_ref[v, w] * slope[w] for w in range(NV)])
                - damping * (outer[v] + inner[v])
                + tile(moved, v, t)
            )


def from_lines(lines_ref, out_ref):
    lane = lax.broadcasted_iota(jnp.int32, (LANES // 2, LANES), 1)
    half = LANES // 2
    for pair in range(NV // 2):
        rows = [
            lines_ref[2 * pair + p, pl.ds(sub, NS, stride=NQ), :]
            for p in range(2)
            for sub in range(NQ)
        ]
        turned = jnp.concatenate(rows, axis=0).T
        top, bottom = turned[:half], turned[half:]
        out_ref[2 * pair] = jnp.where(lane < half, top, pltpu.roll(bottom, half, 1))
        out_ref[2 * pair + 1] = jnp.where(lane < half, pltpu.roll(top, half, 1), bottom)


def solve_kernel(
    timed_ref,
    local_ref,
    select_ref,
    factor_ref,
    a_ref,
    b_ref,
    phi_ref,
    omega_ref,
    up_ref,
    down_ref,
    residual_ref,
    correction_ref,
    lines_ref,
):
    moved = to_lines(select_ref[...], timed_ref[...])
    sweep = []
    for t in range(NS):
        residual = []
        for v in range(NV):
            value = (
                moved[t * NQ : (t + 1) * NQ, v * LANES : (v + 1) * LANES] + local_ref[v, t]
            )
            lines_ref[v, t * NQ : (t + 1) * NQ] = value
            residual.append(value)
        value = applied(factor_ref, (t,), residual)
        if t > 0:
            before = applied(a_ref, (t,), sweep[t - 1])
            value = [x + y for x, y in zip(value, before)]
        sweep.append(value)
    from_lines(lines_ref, residual_ref)

    carry = sweep[NS - 1]
    for step in range(LEVELS):
        more = applied(up_ref, (step,), [shift_chunks(x, 2**step) for x in carry])
        carry = [x + y for x, y in zip(carry, more)]
    carry = [shift_chunks(x, 1) for x in carry]
    back = [None] * NS
    for t in reversed(range(NS)):
        more = applied(phi_ref, (t,), carry)
        value = [x + y for x, y in zip(sweep[t], more)]
        if t + 1 < NS:
            more = applied(b_ref, (t,), back[t + 1])
            value = [x + y for x, y in zip(value, more)]
        back[t] = value
    carry = back[0]
    for step in range(LEVELS):
        more = applied(down_ref, (step,), [shift_chunks(x, -(2**step)) for x in carry])
        carry = [x + y for x, y in zip(carry, more)]
    carry = [shift_chunks(x, -1) for x in carry]
    for t in range(NS):
        more = applied(omega_ref, (t,), carry)
        for v in range(NV):
            lines_ref[v, t * NQ : (t + 1) * NQ] = back[t][v] + more[v]
    from_lines(lines_ref, correction_ref)


VMEM = pl.BlockSpec(memory_space=pltpu.VMEM)
SMEM = pl.BlockSpec(memory_space=pltpu.SMEM)
MIB = 2**20


def f32(*shape):
    return jax.ShapeDtypeStruct(shape, jnp.float32)


def call(body, outs, specs, operands, limit, flops, scratch=()):
    moved = sum(x.size * x.dtype.itemsize for x in operands)
    moved += sum(4 * o.size for o in outs)
    return pl.pallas_call(
        body,
        out_shape=outs,
        in_specs=specs,
        out_specs=[VMEM] * len(outs),
        scratch_shapes=list(scratch),
        compiler_params=pltpu.CompilerParams(vmem_limit_bytes=limit * MIB),
        cost_estimate=pl.CostEstimate(flops=flops, bytes_accessed=moved, transcendentals=0),
    )(*operands)


def shards(
    flow_state,
    forcing,
    pivot_table,
    block_offset,
    line_perm,
    axial_jac,
    radial_jac,
    lower_block,
    upper_block,
):
    hp = lax.Precision.HIGHEST
    state = flow_state[0]
    count = lax.axis_size("inst")
    variables, stations, radial = state.shape
    share = variables * stations // count

    gathered = lax.all_to_all(
        state.reshape(count, share // 4, 4, radial), "inst", 0, 0, tiled=True
    )
    (timed,) = call(
        time_kernel,
        [f32(count * share, radial)],
        [VMEM, VMEM],
        [spectral_matrix(count), gathered.reshape(count * share, radial)],
        4,
        2 * count * count * share * radial,
    )
    timed = lax.all_to_all(
        timed.reshape(count, share // 4, 4, radial), "inst", 0, 0, tiled=True
    ).reshape(variables, stations, radial)

    chips = lax.axis_size("space")
    up = [(i, i + 1) for i in range(chips - 1)]
    low = lax.ppermute(state[:, stations - 1], "space", up)
    high = lax.ppermute(state[:, 0], "space", [(target, source) for source, target in up])

    table = pivot_table.reshape(KB, NV * NV, NH, NQ, NS).transpose(1, 4, 3, 2, 0)
    chosen = (block_offset[None] == lax.broadcasted_iota(jnp.int32, (KB, stations), 0)).astype(
        jnp.float32
    )
    blank = jnp.zeros_like(chosen)
    chosen = jnp.concatenate(
        [jnp.concatenate([chosen, blank], 1), jnp.concatenate([blank, chosen], 1)], 0
    )
    factor = jnp.dot(table.reshape(-1, NH * KB), chosen, precision=hp)
    factor = factor.reshape(NV * NV, NS, NQ, LANES)
    order = line_perm.reshape(NH, NQ, NS).transpose(2, 1, 0).reshape(NS * NQ, NH, 1)
    select = order == lax.broadcasted_iota(jnp.int32, (NS * NQ, NH, radial), 2)
    select = select.astype(jnp.bfloat16).reshape(NS * NQ, NH * radial)

    coef = f32(NV * NV, NS, NQ, LANES)
    level = f32(NV * NV, LEVELS, NQ, LANES)
    tables = call(
        tables_kernel,
        [coef, coef, coef, coef, level, level],
        [VMEM, SMEM, SMEM],
        [factor, lower_block, upper_block],
        12,
        36 * 6 * 2 * 1024 * 40,
    )
    (local,) = call(
        local_kernel,
        [f32(NV, NS, NQ, LANES)],
        [VMEM, VMEM, VMEM, VMEM, VMEM, SMEM, SMEM],
        [state, forcing[0], low, high, select, axial_jac, radial_jac],
        8,
        2 * 768 * 64 * 256 * 6,
    )
    residual, correction = call(
        solve_kernel,
        [f32(variables, stations, radial)] * 2,
        [VMEM] * 10,
        [timed, local, select, factor, *tables],
        16,
        36 * 2 * 1024 * 50,
        [pltpu.VMEM((NV, NS * NQ, LANES), jnp.float32)],
    )
    return residual[None], correction[None]


def solution(mesh):
    return jax.shard_map(
        shards,
        mesh=mesh,
        in_specs=(
            P("inst", None, "space", None),
            P("inst", None, "space", None),
            P(),
            P("space"),
            P(),
            P(),
            P(),
            P(),
            P(),
        ),
        out_specs=(P("inst", None, "space", None), P("inst", None, "space", None)),
        check_vma=False,
    )
```

profile of v0, /device:TPU:7, one launch (start us, length us, event | category | flops | bytes accessed | tf_op | source)
XLA Modules:
  0.0 61.0 jit_solution(13485828134749896429)
XLA Ops:
  0.6 9.5 %all-to-all-start = ((f32[32,3,4,128]{3,2,1,0:T(4,128)}), f32[32,3,4,128]{3,2,1,0:T(4,128)S(1)}, u32[]{:S(2)}, u32[]{:S(2)}) async-start(f32[32,3,4,128]{3,2,1,0:T(4,128)} %bitcast.39), calls=%async_computation | async-start | bytes 393216 | tf_op jit(solution)/shard_map/all_to_all | solution.py:312
  10.2 1.1 %copy.30 = f32[1,6,64,128]{3,1,2,0:T(8,128)S(1)} copy(f32[1,6,64,128]{3,2,1,0:T(8,128)} %param.9) | data formatting | bytes 393216 | tf_op args[0]
  11.8 2.4 %collective-permute-start.1 = (f32[6,128]{1,0:T(8,128)}, f32[6,128]{1,0:T(8,128)S(1)}, u32[]{:S(2)}, u32[]{:S(2)}) collective-permute-start(f32[6,128]{1,0:T(8,128)} %get-tuple-element.18), channel_id=1, source_target_pairs={{1,0},{2,1},{3,2},{4,3},{5,4},{6,5},{7,6},{8,7},{9,8},{10,9},{11,1... | collective-permute-start | bytes 9224 | tf_op jit(solution)/shard_map/ppermute | solution.py:330
  14.3 8.8 %collective-permute-start = (f32[6,128]{1,0:T(8,128)}, f32[6,128]{1,0:T(8,128)S(1)}, u32[]{:S(2)}, u32[]{:S(2)}) collective-permute-start(f32[6,128]{1,0:T(8,128)} %get-tuple-element.19), channel_id=1, source_target_pairs={{0,1},{1,2},{2,3},{3,4},{4,5},{5,6},{6,7},{7,8},{8,9},{9,10},{10,1... | collective-permute-start | bytes 9224 | tf_op jit(solution)/shard_map/ppermute | solution.py:329
  23.3 1.0 %shard_map.104 = f32[384,128]{1,0:T(8,128)} custom-call(f32[32,32]{1,0:T(8,128)S(1)} %multiply_subtract_fusion.spectral_ref, f32[384,128]{1,0:T(8,128)S(1)} %bitcast.41), custom_call_target="tpu_custom_call" | custom-call | flops 3145728 | bytes 397312 | tf_op jit(solution)/shard_map/pallas_call | solution.py:284
  24.2 8.3 %all-to-all-start.1 = ((f32[32,3,4,128]{3,2,1,0:T(4,128)}), f32[32,3,4,128]{3,2,1,0:T(4,128)}, u32[]{:S(2)}, u32[]{:S(2)}) async-start(f32[32,3,4,128]{3,2,1,0:T(4,128)} %bitcast.2), calls=%async_computation.1 | async-start | bytes 393216 | tf_op jit(solution)/shard_map/all_to_all | solution.py:323
  32.8 2.7 %reshape.35 = f32[8,36,2,8,8]{4,3,2,0,1:T(8,128)} reshape(f32[8,6,6,128]{3,0,2,1:T(8,128)S(1)} %copy-done.18) | data formatting | bytes 294912 | tf_op jit(solution)/shard_map/reshape | solution.py:332
  35.5 2.0 %copy.20 = f32[36,8,8,2,8]{2,1,0,4,3:T(8,128)S(1)} copy(f32[36,8,8,2,8]{1,2,3,4,0:T(8,128)} %bitcast.43) | data formatting | bytes 294912 | tf_op jit(solution)/shard_map/transpose | solution.py:332
  37.5 1.3 %reshape.36 = f32[2304,16]{0,1:T(8,128)S(1)} reshape(f32[36,8,8,2,8]{2,1,0,4,3:T(8,128)S(1)} %copy.20) | data formatting | bytes 294912 | tf_op jit(solution)/shard_map/reshape | solution.py:340
  38.9 1.2 %convolution_bitcast_fusion = f32[2304,128]{0,1:T(8,128)S(1)} fusion(f32[2304,16]{0,1:T(8,128)S(1)} %reshape.36, f32[8,64]{1,0:T(8,128)S(1)} %fusion.14), kind=kOutput, calls=%fused_computation | convolution fusion | flops 56633344 | bytes 1329152 | tf_op jit(solution)/shard_map/dot_general | solution.py:340
  41.5 3.4 %shard_map.106 = (f32[36,8,8,128]{3,2,1,0:T(8,128)S(1)}, f32[36,8,8,128]{3,2,1,0:T(8,128)S(1)}, f32[36,8,8,128]{3,2,1,0:T(8,128)S(1)}, f32[36,8,8,128]{3,2,1,0:T...) custom-call(f32[36,8,8,128]{3,2,1,0:T(8,128)S(1)} %bitcast.37, f32[6,6]{1,0:T(8,128)S(1)} %copy-done.14, ...), custom_call_target="tpu_custom_call" | custom-call | flops 17694720 | bytes 7078176 | tf_op jit(solution)/shard_map/pallas_call | solution.py:284
  45.0 1.0 %copy-done.1 = f32[36,8,8,128]{3,2,1,0:T(8,128)} copy-done((f32[36,8,8,128]{3,2,1,0:T(8,128)}, f32[36,8,8,128]{3,2,1,0:T(8,128)S(1)}, u32[]{:S(2)}) %copy-start.1) | copy-done | bytes 1179672
  46.0 1.0 %copy-done.3 = f32[36,8,8,128]{3,2,1,0:T(8,128)} copy-done((f32[36,8,8,128]{3,2,1,0:T(8,128)}, f32[36,8,8,128]{3,2,1,0:T(8,128)S(1)}, u32[]{:S(2)}) %copy-start.3) | copy-done | bytes 1179672
  47.0 0.8 %copy-done.7 = f32[36,4,8,128]{3,2,1,0:T(8,128)} copy-done((f32[36,4,8,128]{3,2,1,0:T(8,128)}, f32[36,4,8,128]{3,2,1,0:T(8,128)S(1)}, u32[]{:S(2)}) %copy-start.7) | copy-done | bytes 589848
  47.8 0.8 %copy-done.9 = f32[36,4,8,128]{3,2,1,0:T(8,128)} copy-done((f32[36,4,8,128]{3,2,1,0:T(8,128)}, f32[36,4,8,128]{3,2,1,0:T(8,128)S(1)}, u32[]{:S(2)}) %copy-start.9) | copy-done | bytes 589848
  48.7 1.6 %shard_map.105.local_ref = f32[6,8,8,128]{3,2,1,0:T(8,128)S(1)} custom-call(f32[6,64,128]{2,1,0:T(8,128)S(1)} %bitcast.40, f32[6,64,128]{2,1,0:T(8,128)S(1)} %bitcast.42, f32[6,128]{1,0:T(8,128)S(1)} %collective-permute-done.low_ref, f32[6,128]{1,0:T(8,128)S(1)} %collective-permute-done.1.high_ref, bf16[64,256]{1,0:T(8,128)(2,1)S(1)} %copy-done.11, ...), custom_call_target="tpu_custom_call" | custom-call | flops 150994944 | bytes 629024 | tf_op jit(solution)/shard_map/pallas_call | solution.py:284
  50.3 0.7 %copy-done.5 = f32[6,8,8,128]{3,2,1,0:T(8,128)} copy-done((f32[6,8,8,128]{3,2,1,0:T(8,128)}, f32[6,8,8,128]{3,2,1,0:T(8,128)S(1)}, u32[]{:S(2)}) %copy-start.5) | copy-done | bytes 196632
  51.0 1.3 %copy-done.2 = f32[36,8,8,128]{3,2,1,0:T(8,128)S(1)} copy-done((f32[36,8,8,128]{3,2,1,0:T(8,128)S(1)}, f32[36,8,8,128]{3,2,1,0:T(8,128)}, u32[]{:S(2)}) %copy-start.2) | copy-done | bytes 1179672
  52.2 1.3 %copy-done.4 = f32[36,8,8,128]{3,2,1,0:T(8,128)S(1)} copy-done((f32[36,8,8,128]{3,2,1,0:T(8,128)S(1)}, f32[36,8,8,128]{3,2,1,0:T(8,128)}, u32[]{:S(2)}) %copy-start.4) | copy-done | bytes 1179672
  53.5 0.9 %copy-done.6 = f32[6,8,8,128]{3,2,1,0:T(8,128)S(1)} copy-done((f32[6,8,8,128]{3,2,1,0:T(8,128)S(1)}, f32[6,8,8,128]{3,2,1,0:T(8,128)}, u32[]{:S(2)}) %copy-start.6) | copy-done | bytes 196632
  54.4 1.1 %copy-done.8 = f32[36,4,8,128]{3,2,1,0:T(8,128)S(1)} copy-done((f32[36,4,8,128]{3,2,1,0:T(8,128)S(1)}, f32[36,4,8,128]{3,2,1,0:T(8,128)}, u32[]{:S(2)}) %copy-start.8) | copy-done | bytes 589848
  55.5 1.1 %copy-done.10 = f32[36,4,8,128]{3,2,1,0:T(8,128)S(1)} copy-done((f32[36,4,8,128]{3,2,1,0:T(8,128)S(1)}, f32[36,4,8,128]{3,2,1,0:T(8,128)}, u32[]{:S(2)}) %copy-start.10) | copy-done | bytes 589848
  56.6 0.8 %copy-done.12 = bf16[64,256]{1,0:T(8,128)(2,1)S(1)} copy-done((bf16[64,256]{1,0:T(8,128)(2,1)S(1)}, bf16[64,256]{1,0:T(8,128)(2,1)}, u32[]{:S(2)}) %copy-start.12) | copy-done | bytes 32792
  57.3 3.7 %shard_map.107 = (f32[6,64,128]{2,1,0:T(8,128)}, f32[6,64,128]{2,1,0:T(8,128)}) custom-call(f32[6,64,128]{2,1,0:T(8,128)} %bitcast.3.timed_ref, f32[6,8,8,128]{3,2,1,0:T(8,128)S(1)} %copy-done.6, bf16[64,256]{1,0:T(8,128)(2,1)S(1)} %copy-done.12, f32[36,8,8,128]{3,2,1,0:T(8,128)S(1)} %bitcast.38, f32[36,8,8,128]{3,2,1,0:T(8,128)S(1)} %get-tuple-element.10.a_ref, ...), custom_call_target="tpu_custom_call" | custom-call | flops 3686400 | bytes 7897088 | tf_op jit(solution)/shard_map/pallas_call | solution.py:284
  (44 shorter events, 2.4 us)
Async XLA Ops:
  0.6 31.9 %copy-start.19 = (s32[128]{0:T(128)S(1)}, s32[128]{0:T(128)}, u32[]{:S(2)}) copy-start(s32[128]{0:T(128)} %param.13) | copy-start | bytes 1540
  0.6 32.1 %copy-start.18 = (f32[8,6,6,128]{3,0,2,1:T(8,128)S(1)}, f32[8,6,6,128]{3,0,2,1:T(8,128)}, u32[]{:S(2)}) copy-start(f32[8,6,6,128]{3,0,2,1:T(8,128)} %param.11) | copy-start | bytes 442372
  0.6 22.6 %all-to-all-start = ((f32[32,3,4,128]{3,2,1,0:T(4,128)}), f32[32,3,4,128]{3,2,1,0:T(4,128)S(1)}, u32[]{:S(2)}, u32[]{:S(2)}) async-start(f32[32,3,4,128]{3,2,1,0:T(4,128)} %bitcast.39), calls=%async_computation | async-start | bytes 393216 | tf_op jit(solution)/shard_map/all_to_all | solution.py:312
  11.8 36.8 %collective-permute-start.1 = (f32[6,128]{1,0:T(8,128)}, f32[6,128]{1,0:T(8,128)S(1)}, u32[]{:S(2)}, u32[]{:S(2)}) collective-permute-start(f32[6,128]{1,0:T(8,128)} %get-tuple-element.18), channel_id=1, source_target_pairs={{1,0},{2,1},{3,2},{4,3},{5,4},{6,5},{7,6},{8,7},{9,8},{10,9},{11,1... | collective-permute-start | bytes 9224 | tf_op jit(solution)/shard_map/ppermute | solution.py:330
  14.3 34.4 %collective-permute-start = (f32[6,128]{1,0:T(8,128)}, f32[6,128]{1,0:T(8,128)S(1)}, u32[]{:S(2)}, u32[]{:S(2)}) collective-permute-start(f32[6,128]{1,0:T(8,128)} %get-tuple-element.19), channel_id=1, source_target_pairs={{0,1},{1,2},{2,3},{3,4},{4,5},{5,6},{6,7},{7,8},{8,9},{9,10},{10,1... | collective-permute-start | bytes 9224 | tf_op jit(solution)/shard_map/ppermute | solution.py:329
  24.2 26.7 %all-to-all-start.1 = ((f32[32,3,4,128]{3,2,1,0:T(4,128)}), f32[32,3,4,128]{3,2,1,0:T(4,128)}, u32[]{:S(2)}, u32[]{:S(2)}) async-start(f32[32,3,4,128]{3,2,1,0:T(4,128)} %bitcast.2), calls=%async_computation.1 | async-start | bytes 393216 | tf_op jit(solution)/shard_map/all_to_all | solution.py:323
  37.5 1.3 %copy-start.20 = (s32[64]{0:T(128)S(1)}, s32[64]{0:T(128)}, u32[]{:S(2)}) copy-start(s32[64]{0:T(128)} %param.12) | copy-start | bytes 772
  40.8 0.7 %copy-start.14 = (f32[6,6]{1,0:T(8,128)S(1)}, f32[6,6]{1,0:T(8,128)}, u32[]{:S(2)}) copy-start(f32[6,6]{1,0:T(8,128)} %lower_ref.1) | copy-start | bytes 436
  40.8 0.7 %copy-start.15 = (f32[6,6]{1,0:T(8,128)S(1)}, f32[6,6]{1,0:T(8,128)}, u32[]{:S(2)}) copy-start(f32[6,6]{1,0:T(8,128)} %upper_ref.1) | copy-start | bytes 436
  41.2 7.5 %copy-start = (f32[1,6,64,128]{3,2,1,0:T(8,128)S(1)}, f32[1,6,64,128]{3,2,1,0:T(8,128)}, u32[]{:S(2)}) copy-start(f32[1,6,64,128]{3,2,1,0:T(8,128)} %param.9) | copy-start | bytes 589828
  41.2 7.5 %copy-start.11 = (bf16[64,256]{1,0:T(8,128)(2,1)S(1)}, bf16[64,256]{1,0:T(8,128)(2,1)}, u32[]{:S(2)}) copy-start(bf16[64,256]{1,0:T(8,128)(2,1)} %fusion.select_ref) | copy-start | bytes 98308
  41.2 7.5 %copy-start.13 = (f32[1,6,64,128]{3,2,1,0:T(8,128)S(1)}, f32[1,6,64,128]{3,2,1,0:T(8,128)}, u32[]{:S(2)}) copy-start(f32[1,6,64,128]{3,2,1,0:T(8,128)} %param.10) | copy-start | bytes 589828
  41.2 7.5 %copy-start.16 = (f32[6,6]{1,0:T(8,128)S(1)}, f32[6,6]{1,0:T(8,128)}, u32[]{:S(2)}) copy-start(f32[6,6]{1,0:T(8,128)} %axial_ref.1) | copy-start | bytes 436
  41.2 7.5 %copy-start.17 = (f32[6,6]{1,0:T(8,128)S(1)}, f32[6,6]{1,0:T(8,128)}, u32[]{:S(2)}) copy-start(f32[6,6]{1,0:T(8,128)} %radial_ref.1) | copy-start | bytes 436
  45.0 1.0 %copy-start.1 = (f32[36,8,8,128]{3,2,1,0:T(8,128)}, f32[36,8,8,128]{3,2,1,0:T(8,128)S(1)}, u32[]{:S(2)}) copy-start(f32[36,8,8,128]{3,2,1,0:T(8,128)S(1)} %get-tuple-element.12.phi_ref) | copy-start | bytes 3538948
  46.0 1.0 %copy-start.3 = (f32[36,8,8,128]{3,2,1,0:T(8,128)}, f32[36,8,8,128]{3,2,1,0:T(8,128)S(1)}, u32[]{:S(2)}) copy-start(f32[36,8,8,128]{3,2,1,0:T(8,128)S(1)} %get-tuple-element.13.omega_ref) | copy-start | bytes 3538948
  47.0 0.8 %copy-start.7 = (f32[36,4,8,128]{3,2,1,0:T(8,128)}, f32[36,4,8,128]{3,2,1,0:T(8,128)S(1)}, u32[]{:S(2)}) copy-start(f32[36,4,8,128]{3,2,1,0:T(8,128)S(1)} %get-tuple-element.14.up_ref) | copy-start | bytes 1769476
  47.8 0.8 %copy-start.9 = (f32[36,4,8,128]{3,2,1,0:T(8,128)}, f32[36,4,8,128]{3,2,1,0:T(8,128)S(1)}, u32[]{:S(2)}) copy-start(f32[36,4,8,128]{3,2,1,0:T(8,128)S(1)} %get-tuple-element.15.down_ref) | copy-start | bytes 1769476
  50.9 1.3 %copy-start.2 = (f32[36,8,8,128]{3,2,1,0:T(8,128)S(1)}, f32[36,8,8,128]{3,2,1,0:T(8,128)}, u32[]{:S(2)}) copy-start(f32[36,8,8,128]{3,2,1,0:T(8,128)} %copy-done.1) | copy-start | bytes 3538948
  52.2 1.3 %copy-start.4 = (f32[36,8,8,128]{3,2,1,0:T(8,128)S(1)}, f32[36,8,8,128]{3,2,1,0:T(8,128)}, u32[]{:S(2)}) copy-start(f32[36,8,8,128]{3,2,1,0:T(8,128)} %copy-done.3) | copy-start | bytes 3538948
  53.5 0.9 %copy-start.6 = (f32[6,8,8,128]{3,2,1,0:T(8,128)S(1)}, f32[6,8,8,128]{3,2,1,0:T(8,128)}, u32[]{:S(2)}) copy-start(f32[6,8,8,128]{3,2,1,0:T(8,128)} %copy-done.5) | copy-start | bytes 589828
  54.4 1.1 %copy-start.8 = (f32[36,4,8,128]{3,2,1,0:T(8,128)S(1)}, f32[36,4,8,128]{3,2,1,0:T(8,128)}, u32[]{:S(2)}) copy-start(f32[36,4,8,128]{3,2,1,0:T(8,128)} %copy-done.7) | copy-start | bytes 1769476
  55.5 1.1 %copy-start.10 = (f32[36,4,8,128]{3,2,1,0:T(8,128)S(1)}, f32[36,4,8,128]{3,2,1,0:T(8,128)}, u32[]{:S(2)}) copy-start(f32[36,4,8,128]{3,2,1,0:T(8,128)} %copy-done.9) | copy-start | bytes 1769476
  56.5 0.8 %copy-start.12 = (bf16[64,256]{1,0:T(8,128)(2,1)S(1)}, bf16[64,256]{1,0:T(8,128)(2,1)}, u32[]{:S(2)}) copy-start(bf16[64,256]{1,0:T(8,128)(2,1)} %fusion.select_ref) | copy-start | bytes 98308
  (1 other events, 0.7 us)
where the time goes:
time: 61.8 us; the launch traced here: 61 us
  starting transfers between devices  29.1 us (47%)
  local copies, waits for them, and re-layouts  19.5 us (32%)
  Pallas kernels  9.66 us (16%)
  matrix products  1.19 us (2%)
  between operations  0.87 us (1%)
  other arithmetic  0.73 us (1%)
    unnamed x43, local copies, waits for them, and re-layouts  12.1 us
    pallas_call x4, Pallas kernels, call(): pl.pallas_call(body, out_shape=outs, in_specs=specs, out_specs=[VMEM] * l...  9.66 us
    all_to_all x1, starting transfers between devices, shards(): lax.all_to_all(state.reshape(count, share // 4, 4, radial), 'inst', 0, 0,...  9.51 us
    ppermute x1, starting transfers between devices, shards(): low = lax.ppermute(state[:, stations - 1], 'space', up)  8.84 us
    all_to_all x1, starting transfers between devices, shards(): lax.all_to_all(timed.reshape(count, share // 4, 4, radial), 'inst', 0, 0,...  8.29 us
    reshape x1, local copies, waits for them, and re-layouts, shards(): pivot_table.reshape(KB, NV * NV, NH, NQ, NS).transpose(1, 4, 3, 2, 0)  2.71 us
    ppermute x1, starting transfers between devices, shards(): lax.ppermute(state[:, 0], 'space', [(target, source) for source, target i...  2.44 us
    transpose x1, local copies, waits for them, and re-layouts, shards(): pivot_table.reshape(KB, NV * NV, NH, NQ, NS).transpose(1, 4, 3, 2, 0)  2.03 us
  transfers between devices with their start and end apart: 4, of which 0 were waited for; matrix products, arithmetic and copies ran while one was open for 17% of the time, Pallas kernels for 10%

commit v1 on v0

v1 whole, which is shorter than its diff:
```python
import jax
import jax.numpy as jnp
from jax import lax
from jax.experimental import pallas as pl
from jax.experimental.pallas import tpu as pltpu
from jax.sharding import PartitionSpec as P

frequency = 0.5
viscosity = 0.01
damping = 0.25

NV = 6
NQ = 8
NS = 8
NH = 2
KB = 8
LANES = 128
LEVELS = 4


def spectral_matrix(count):
    row_index = lax.broadcasted_iota(jnp.int32, (count, count), 0)
    col_index = lax.broadcasted_iota(jnp.int32, (count, count), 1)
    distance = row_index - col_index
    parity = (1 - 2 * jnp.mod(distance, 2)).astype(jnp.float32)
    phase_angle = jnp.pi * distance.astype(jnp.float32) / count
    diagonal_mask = distance == 0
    sine_value = jnp.where(diagonal_mask, 1.0, jnp.sin(phase_angle))
    first_order = jnp.where(diagonal_mask, 0.0, 0.5 * parity * jnp.cos(phase_angle) / sine_value)
    second_order = jnp.where(
        diagonal_mask, -(count * count + 2) / 12.0, -0.5 * parity / (sine_value * sine_value)
    )
    return frequency * first_order - viscosity * second_order


def shift_chunks(tile, amount):
    sub = lax.broadcasted_iota(jnp.int32, tile.shape, 0)
    lane = lax.broadcasted_iota(jnp.int32, tile.shape, 1)
    zero = jnp.zeros_like(tile)
    swapped = pltpu.roll(tile, LANES // 2, 1)
    if amount == NQ:
        return jnp.where(lane >= LANES // 2, swapped, zero)
    if amount == -NQ:
        return jnp.where(lane < LANES // 2, swapped, zero)
    near = pltpu.roll(tile, amount % NQ, 0)
    far = pltpu.roll(swapped, amount % NQ, 0)
    if amount > 0:
        return jnp.where(sub >= amount, near, jnp.where(lane >= LANES // 2, far, zero))
    return jnp.where(sub < NQ + amount, near, jnp.where(lane < LANES // 2, far, zero))


def product(left, right):
    return [
        [sum_of([left[v][x] * right[x][w] for x in range(NV)]) for w in range(NV)]
        for v in range(NV)
    ]


def sum_of(terms):
    while len(terms) > 1:
        terms = [
            terms[i] + terms[i + 1] if i + 1 < len(terms) else terms[i]
            for i in range(0, len(terms), 2)
        ]
    return terms[0]


def applied(coef_ref, index, vector):
    return [
        sum_of([coef_ref[(v * NV + w, *index)] * vector[w] for w in range(NV)]) for v in range(NV)
    ]


def split(value):
    high = value.astype(jnp.bfloat16)
    rest = value - high.astype(jnp.float32)
    middle = rest.astype(jnp.bfloat16)
    return high, middle, (rest - middle.astype(jnp.float32)).astype(jnp.bfloat16)


def picked(select, value):
    dims = (((1,), (1,)), ((), ()))
    parts = [
        lax.dot_general(select, part, dims, preferred_element_type=jnp.float32)
        for part in split(value)
    ]
    return parts[0] + parts[1] + parts[2]


def doubled(planes):
    blank = jnp.zeros_like(planes[0])
    blocks = []
    for plane in planes:
        blocks.append(jnp.concatenate([plane, blank], axis=1))
        blocks.append(jnp.concatenate([blank, plane], axis=1))
    return jnp.concatenate(blocks, axis=0)


def fetch(pairs, sems):
    copies = [pltpu.make_async_copy(x, y, sems.at[i]) for i, (x, y) in enumerate(pairs)]
    for copy in copies:
        copy.start()
    return copies


def prepare_kernel(*refs):
    table_hbm, offset_hbm, order_hbm, state_hbm, forcing_hbm = refs[:5]
    lower_ref, upper_ref, axial_ref, radial_ref = refs[5:9]
    factor_ref, a_ref, up_ref, local_ref, select_ref, b_out, down_out = refs[9:16]
    table_ref, offset_ref, order_ref, state_ref, forcing_ref = refs[16:21]
    b_ref, down_ref, turned_ref, sems, b_sem, down_sem = refs[21:]
    copies = fetch(
        [
            (order_hbm, order_ref),
            (offset_hbm, offset_ref),
            (table_hbm, table_ref),
            (state_hbm, state_ref),
            (forcing_hbm, forcing_ref),
        ],
        sems,
    )
    for copy in copies[:3]:
        copy.wait()
    slot = lax.broadcasted_iota(jnp.int32, (LANES, LANES), 0)
    turned_ref[...] = (slot == order_ref[...]).astype(jnp.float32).T
    halves = [
        jnp.concatenate(
            [turned_ref[pl.ds(half * NS * NQ + t, NQ, stride=NS), :] for t in range(NS)], axis=0
        )
        for half in range(NH)
    ]
    select = jnp.concatenate(halves, axis=1).astype(jnp.bfloat16)
    select_ref[...] = select

    tables = [[table_ref[v * NV + w] for w in range(NV)] for v in range(NV)]
    lower = [[-lower_ref[v, w] for w in range(NV)] for v in range(NV)]
    upper = [[-upper_ref[v, w] for w in range(NV)] for v in range(NV)]
    row = lax.broadcasted_iota(jnp.int32, (NS * NQ, NH * LANES), 0)
    column = lax.broadcasted_iota(jnp.int32, (NS * NQ, NH * LANES), 1)
    place = (row % NQ) * NS + row // NQ
    place = jnp.where(column < LANES, place, place + LANES + NS * NQ)
    lines = (column == place).astype(jnp.bfloat16)
    lane = lax.broadcasted_iota(jnp.int32, (NS * NQ, LANES), 1)
    offset = jnp.concatenate([offset_ref[...], offset_ref[...]], axis=1)
    index = jnp.where(lane < LANES // 2, 0, KB) + offset
    group = LANES // (NH * KB)

    def spread(value, ref):
        planes = [e for line in value for e in line]
        padding = [jnp.zeros_like(planes[0])] * (-len(planes) % group)
        moved = picked(lines, doubled(planes + padding))
        for i in range(NV * NV):
            start = i // group * LANES
            source = moved[:, start : start + LANES]
            chosen = jnp.take_along_axis(source, index + (i % group) * NH * KB, axis=1)
            for t in range(NS):
                ref[i, t] = chosen[t * NQ : (t + 1) * NQ]

    def load(ref, t):
        return [[ref[v * NV + w, t] for w in range(NV)] for v in range(NV)]

    def keep(ref, t, value):
        for v in range(NV):
            for w in range(NV):
                ref[v * NV + w, t] = value[v][w]

    spread(product(tables, upper), b_ref)
    spread(product(tables, lower), a_ref)
    spread(tables, factor_ref)
    stores = fetch([(b_ref, b_out)], b_sem)
    keep(up_ref, 0, load(a_ref, 0))
    keep(down_ref, 0, load(b_ref, NS - 1))

    def extend(t, carry):
        keep(up_ref, 0, product(load(a_ref, t), load(up_ref, 0)))
        keep(down_ref, 0, product(load(b_ref, NS - 1 - t), load(down_ref, 0)))
        return carry

    lax.fori_loop(1, NS, extend, 0)
    for ref, sign in ((up_ref, 1), (down_ref, -1)):
        for step in range(1, LEVELS):
            level = load(ref, step - 1)
            moved = [[shift_chunks(e, sign * 2 ** (step - 1)) for e in line] for line in level]
            keep(ref, step, product(level, moved))

    stores += fetch([(down_ref, down_out)], down_sem)
    for copy in copies[3:]:
        copy.wait()
    stations = state_ref.shape[1]
    row = lax.broadcasted_iota(jnp.int32, (stations, LANES), 0)
    state = [state_ref[v] for v in range(NV)]
    ahead = [
        jnp.where(row == stations - 1, 0.0, pltpu.roll(state[v], stations - 1, 0))
        for v in range(NV)
    ]
    behind = [jnp.where(row == 0, 0.0, pltpu.roll(state[v], 1, 0)) for v in range(NV)]
    slope = [0.5 * (ahead[v] - behind[v]) for v in range(NV)]
    direct = [
        sum_of([axial_ref[v, w] * slope[w] for w in range(NV)])
        - damping * (ahead[v] + behind[v] - 4.0 * state[v])
        - forcing_ref[v]
        for v in range(NV)
    ]
    lines = picked(select, doubled(state))
    moved = picked(select, doubled(direct))

    def tile(array, v, t):
        return array[t * NQ : (t + 1) * NQ, v * LANES : (v + 1) * LANES]

    for t in range(NS):
        outer = [
            tile(lines, v, t + 1) if t + 1 < NS else shift_chunks(tile(lines, v, 0), -1)
            for v in range(NV)
        ]
        inner = [
            tile(lines, v, t - 1) if t > 0 else shift_chunks(tile(lines, v, NS - 1), 1)
            for v in range(NV)
        ]
        slope = [0.5 * (outer[v] - inner[v]) for v in range(NV)]
        for v in range(NV):
            local_ref[v, t] = (
                sum_of([radial_ref[v, w] * slope[w] for w in range(NV)])
                - damping * (outer[v] + inner[v])
                + tile(moved, v, t)
            )
    for copy in stores:
        copy.wait()


def time_kernel(spectral_ref, state_ref, timed_hbm, timed_ref, sem):
    count = spectral_ref.shape[0]
    rows = state_ref.shape[0] // count
    high, middle, low = split(spectral_ref[...])
    weight = jnp.concatenate([high, high, middle, high, low, middle], axis=1)
    stacked = jnp.concatenate(
        [state_ref[pl.ds(row, count, stride=rows), :] for row in range(rows)], axis=1
    )
    high, middle, low = split(stacked)
    result = jnp.dot(
        weight,
        jnp.concatenate([high, middle, high, low, high, middle], axis=0),
        preferred_element_type=jnp.float32,
    )
    for row in range(rows):
        timed_ref[pl.ds(row, count, stride=rows), :] = result[:, row * LANES : (row + 1) * LANES]
    copy = pltpu.make_async_copy(timed_ref, timed_hbm, sem)
    copy.start()
    copy.wait()


def from_lines(lines_ref, out_ref, out_hbm, sems):
    lane = lax.broadcasted_iota(jnp.int32, (LANES // 2, LANES), 1)
    half = LANES // 2
    copies = []
    for pair in range(NV // 2):
        rows = [
            lines_ref[2 * pair + p, pl.ds(sub, NS, stride=NQ), :]
            for p in range(2)
            for sub in range(NQ)
        ]
        turned = jnp.concatenate(rows, axis=0).T
        top, bottom = turned[:half], turned[half:]
        out_ref[2 * pair] = jnp.where(lane < half, top, pltpu.roll(bottom, half, 1))
        out_ref[2 * pair + 1] = jnp.where(lane < half, pltpu.roll(top, half, 1), bottom)
        both = pl.ds(2 * pair, 2)
        copies.append(pltpu.make_async_copy(out_ref.at[both], out_hbm.at[both], sems.at[pair]))
        copies[-1].start()
    return copies


def solve_kernel(*refs):
    timed_ref, select_ref, local_ref, factor_ref, a_ref, up_ref, swap_ref, other_ref = refs[:8]
    b_hbm, down_hbm, parity_ref, axial_ref, residual_hbm, correction_hbm = refs[8:14]
    joined_ref, b_ref, down_ref, residual_ref, correction_ref, lines_ref = refs[14:20]
    sems, residual_sems, correction_sems = refs[20:]
    loads = fetch([(b_hbm, b_ref), (down_hbm, down_ref)], sems)
    even = parity_ref[0] == 0
    high = [jnp.where(even, swap_ref[v, 0, :1], other_ref[v, 0, :1]) for v in range(NV)]
    low = [
        jnp.where(even, other_ref[v, 1, NQ - 1 :], swap_ref[v, 1, NQ - 1 :])
        for v in range(NV)
    ]
    row = lax.broadcasted_iota(jnp.int32, (NQ, LANES), 0)
    stations = timed_ref.shape[1]
    for v in range(NV):
        before = sum_of([-0.5 * axial_ref[v, w] * low[w] for w in range(NV)]) - damping * low[v]
        after = sum_of([0.5 * axial_ref[v, w] * high[w] for w in range(NV)]) - damping * high[v]
        joined_ref[v, :NQ] = timed_ref[v, :NQ] + jnp.where(row == 0, before, 0.0)
        joined_ref[v, NQ : stations - NQ] = timed_ref[v, NQ : stations - NQ]
        joined_ref[v, stations - NQ :] = timed_ref[v, stations - NQ :] + jnp.where(
            row == NQ - 1, after, 0.0
        )
    moved = picked(select_ref[...], doubled([joined_ref[v] for v in range(NV)]))
    own = []
    ends = None
    for t in range(NS):
        residual = []
        for v in range(NV):
            value = (
                moved[t * NQ : (t + 1) * NQ, v * LANES : (v + 1) * LANES] + local_ref[v, t]
            )
            lines_ref[v, t * NQ : (t + 1) * NQ] = value
            residual.append(value)
        value = applied(factor_ref, (t,), residual)
        own.append(value)
        if t > 0:
            value = [x + y for x, y in zip(value, applied(a_ref, (t,), ends))]
        ends = value
    copies = from_lines(lines_ref, residual_ref, residual_hbm, residual_sems)

    for step in range(LEVELS):
        more = applied(up_ref, (step,), [shift_chunks(x, 2**step) for x in ends])
        ends = [x + y for x, y in zip(ends, more)]
    carry = [shift_chunks(x, 1) for x in ends]
    sweep = []
    for t in range(NS):
        carry = [x + y for x, y in zip(own[t], applied(a_ref, (t,), carry))]
        sweep.append(carry)
    for copy in loads:
        copy.wait()
    ends = sweep[NS - 1]
    for t in reversed(range(NS - 1)):
        ends = [x + y for x, y in zip(sweep[t], applied(b_ref, (t,), ends))]
    for step in range(LEVELS):
        more = applied(down_ref, (step,), [shift_chunks(x, -(2**step)) for x in ends])
        ends = [x + y for x, y in zip(ends, more)]
    carry = [shift_chunks(x, -1) for x in ends]
    for t in reversed(range(NS)):
        carry = [x + y for x, y in zip(sweep[t], applied(b_ref, (t,), carry))]
        for v in range(NV):
            lines_ref[v, t * NQ : (t + 1) * NQ] = carry[v]
    copies += from_lines(lines_ref, correction_ref, correction_hbm, correction_sems)
    for copy in copies:
        copy.wait()


SMEM = pl.BlockSpec(memory_space=pltpu.SMEM)
VMEM = pl.BlockSpec(memory_space=pltpu.VMEM)
MIB = 2**20
ANY = pl.BlockSpec(memory_space=pl.ANY)
PREP = 10**10


def f32(*shape):
    return jax.ShapeDtypeStruct(shape, jnp.float32)


def call(body, near, far, small, near_outs, far_outs, limit, flops, scratch):
    operands = [pltpu.with_memory_space_constraint(x, pltpu.VMEM) for x in near]
    operands += [pltpu.with_memory_space_constraint(x, pltpu.HBM) for x in far]
    outs = [pltpu.VMEM(x.shape, x.dtype) for x in near_outs]
    outs += [pltpu.HBM(x.shape, x.dtype) for x in far_outs]
    moved = sum(x.size * x.dtype.itemsize for x in [*near, *far, *near_outs, *far_outs])
    return pl.pallas_call(
        body,
        out_shape=outs,
        in_specs=[VMEM] * len(near) + [ANY] * len(far) + [SMEM] * len(small),
        out_specs=[VMEM] * len(near_outs) + [ANY] * len(far_outs),
        scratch_shapes=list(scratch),
        compiler_params=pltpu.CompilerParams(vmem_limit_bytes=limit * MIB),
        cost_estimate=pl.CostEstimate(flops=flops, bytes_accessed=moved, transcendentals=0),
    )(*operands, *small)


def shards(
    flow_state,
    forcing,
    pivot_table,
    block_offset,
    line_perm,
    axial_jac,
    radial_jac,
    lower_block,
    upper_block,
):
    state = flow_state[0]
    count = lax.axis_size("inst")
    variables, stations, radial = state.shape
    share = variables * stations // count

    gathered = lax.all_to_all(
        state.reshape(count, share // 4, 4, radial), "inst", 0, 0, tiled=True
    )

    edges = state.reshape(variables, stations // NQ, NQ, radial)
    edges = edges[:, :: stations // NQ - 1]
    chips = lax.axis_size("space")
    swap = lax.ppermute(edges, "space", [(i, i ^ 1) for i in range(chips)])
    other = lax.ppermute(edges, "space", [(i, ((i + 1) ^ 1) - 1) for i in range(1, chips - 1)])
    dma = pltpu.SemaphoreType.DMA

    (timed,) = call(
        time_kernel,
        [spectral_matrix(count), gathered.reshape(count * share, radial)],
        [],
        [],
        [],
        [f32(count * share, radial)],
        8,
        2 * count * count * share * radial,
        [pltpu.VMEM((count * share, radial), jnp.float32), dma],
    )
    timed, state = lax.optimization_barrier((timed, state))
    timed = lax.all_to_all(
        timed.reshape(count, share // 4, 4, radial), "inst", 0, 0, tiled=True
    ).reshape(variables, stations, radial)

    coef = f32(NV * NV, NS, NQ, LANES)
    level = f32(NV * NV, LEVELS, NQ, LANES)
    lines = f32(NV, NS, NQ, LANES)
    one_hot = jax.ShapeDtypeStruct((NS * NQ, NH * LANES), jnp.bfloat16)
    cells = f32(variables, stations, radial)

    def scratch(*shapes):
        return [pltpu.VMEM(x.shape, x.dtype) for x in shapes]

    inputs = [
        pivot_table.transpose(1, 2, 0, 3).reshape(NV * NV, KB, radial),
        block_offset.reshape(1, stations),
        line_perm.reshape(1, radial),
        state,
        forcing[0],
    ]
    factor, a_table, up_table, local, select, b_table, down_table = call(
        prepare_kernel,
        [],
        inputs,
        [lower_block, upper_block, axial_jac, radial_jac],
        [coef, coef, level, lines, one_hot],
        [coef, level],
        16,
        PREP,
        scratch(*inputs, coef, level, f32(LANES, LANES)) + [dma((5,)), dma((1,)), dma((1,))],
    )
    parity = (lax.axis_index("space") % 2).astype(jnp.int32).reshape(1)
    residual, correction = call(
        solve_kernel,
        [timed, select, local, factor, a_table, up_table, swap, other],
        [b_table, down_table],
        [parity, axial_jac],
        [],
        [cells, cells],
        16,
        36 * 2 * 1024 * 50,
        scratch(cells, coef, level, cells, cells)
        + [
            pltpu.VMEM((NV, NS * NQ, LANES), jnp.float32),
            dma((2,)),
            dma((NV // 2,)),
            dma((NV // 2,)),
        ],
    )
    return residual[None], correction[None]


def solution(mesh):
    return jax.shard_map(
        shards,
        mesh=mesh,
        in_specs=(
            P("inst", None, "space", None),
            P("inst", None, "space", None),
            P(),
            P("space"),
            P(),
            P(),
            P(),
            P(),
            P(),
        ),
        out_specs=(P("inst", None, "space", None), P("inst", None, "space", None)),
        check_vma=False,
    )
```

time: 61.8 us -> 46 us (0.74)
  the two profiles are of different devices: /device:TPU:7 before, /device:TPU:5 now
where the time goes in v1:
time: 46 us; the launch traced here: 45.5 us
  starting transfers between devices  29.3 us (64%)
  Pallas kernels  11.4 us (25%)
  waiting for transfers between devices  3.08 us (7%)
  local copies, waits for them, and re-layouts  0.85 us (2%)
  between operations  0.78 us (2%)
    pallas_call x3, Pallas kernels, call(): pl.pallas_call(body, out_shape=outs, in_specs=[VMEM] * len(near) + [ANY]...  11.4 us
    all_to_all x1, starting transfers between devices, shards(): lax.all_to_all(state.reshape(count, share // 4, 4, radial), 'inst', 0, 0,...  9.5 us
    ppermute x1, starting transfers between devices, shards(): swap = lax.ppermute(edges, 'space', [(i, i ^ 1) for i in range(chips)])  9.39 us
    all_to_all x1, starting transfers between devices, shards(): lax.all_to_all(timed.reshape(count, share // 4, 4, radial), 'inst', 0, 0,...  8.26 us
    all_to_all x1, waiting for transfers between devices, shards(): lax.all_to_all(timed.reshape(count, share // 4, 4, radial), 'inst', 0, 0,...  3.08 us
    ppermute x1, starting transfers between devices, shards(): lax.ppermute(edges, 'space', [(i, (i + 1 ^ 1) - 1) for i in range(1, chip...  2.15 us
  transfers between devices with their start and end apart: 4, of which 1 were waited for; matrix products, arithmetic and copies ran while one was open for 2% of the time, Pallas kernels for 17%

profile of v1, /device:TPU:5, one launch (start us, length us, event | category | flops | bytes accessed | tf_op | source)
XLA Modules:
  0.0 45.5 jit_solution(15554346752163357165)
XLA Ops:
  0.6 0.0 copy-start
  0.6 0.0 copy-start.2
  0.7 0.0 copy-start.1
  0.7 0.0 copy-start.3
  0.7 9.5 %all-to-all-start = ((f32[32,3,4,128]{3,2,1,0:T(4,128)}), f32[32,3,4,128]{3,2,1,0:T(4,128)S(1)}, u32[]{:S(2)}, u32[]{:S(2)}) async-start(f32[32,3,4,128]{3,2,1,0:T(4,128)} %bitcast.18), calls=%async_computation | async-start | bytes 393216 | tf_op jit(solution)/shard_map/all_to_all | solution.py:381
  10.2 0.8 %slice.3 = f32[6,2,8,128]{3,2,1,0:T(8,128)S(1)} slice(f32[6,8,8,128]{3,2,1,0:T(8,128)} %bitcast.19), slice={[0:6:1], [0:8:7], [0:8:1], [0:128:1]} | slice | bytes 98304 | tf_op jit(solution)/shard_map/slice | solution.py:386
  11.0 2.2 %collective-permute-start.1 = (f32[6,2,8,128]{3,2,1,0:T(8,128)S(1)}, f32[6,2,8,128]{3,2,1,0:T(8,128)S(1)}, u32[]{:S(2)}, u32[]{:S(2)}) collective-permute-start(f32[6,2,8,128]{3,2,1,0:T(8,128)S(1)} %slice.3), channel_id=1, source_target_pairs={{1,2},{2,1},{3,4},{4,3},{5,6},{6,5},{7,8},{8,7},{9,10},{10,9},{11,... | collective-permute-start | bytes 147464 | tf_op jit(solution)/shard_map/ppermute | solution.py:389
  13.2 9.4 %collective-permute-start = (f32[6,2,8,128]{3,2,1,0:T(8,128)S(1)}, f32[6,2,8,128]{3,2,1,0:T(8,128)S(1)}, u32[]{:S(2)}, u32[]{:S(2)}) collective-permute-start(f32[6,2,8,128]{3,2,1,0:T(8,128)S(1)} %slice.3), channel_id=1, source_target_pairs={{0,1},{1,0},{2,3},{3,2},{4,5},{5,4},{6,7},{7,6},{8,9},{9,8},{10,11... | collective-permute-start | bytes 147464 | tf_op jit(solution)/shard_map/ppermute | solution.py:388
  22.6 0.1 multiply_subtract_fusion.spectral_ref
  22.7 0.0 all-to-all-done
  22.7 1.0 %shard_map.104 = f32[384,128]{1,0:T(8,128)} custom-call(f32[32,32]{1,0:T(8,128)S(1)} %multiply_subtract_fusion.spectral_ref, f32[384,128]{1,0:T(8,128)S(1)} %bitcast.16), custom_call_target="tpu_custom_call" | custom-call | flops 3145728 | bytes 397312 | tf_op jit(solution)/shard_map/pallas_call | solution.py:354
  23.7 8.3 %all-to-all-start.1 = ((f32[32,3,4,128]{3,2,1,0:T(4,128)}), f32[32,3,4,128]{3,2,1,0:T(4,128)S(1)}, u32[]{:S(2)}, u32[]{:S(2)}) async-start(f32[32,3,4,128]{3,2,1,0:T(4,128)} %bitcast.17), calls=%async_computation.1 | async-start | bytes 393216 | tf_op jit(solution)/shard_map/all_to_all | solution.py:404
  31.9 0.0 copy-done
  31.9 0.0 copy-done.2
  32.0 0.0 copy-done.1
  32.0 0.0 copy-done.3
  32.0 6.8 %shard_map.105 = (f32[36,8,8,128]{3,2,1,0:T(8,128)S(1)}, f32[36,8,8,128]{3,2,1,0:T(8,128)S(1)}, f32[36,4,8,128]{3,2,1,0:T(8,128)S(1)}, f32[6,8,8,128]{3,2,1,0:T(...) custom-call(f32[36,8,128]{2,1,0:T(8,128)} %bitcast.24, ...), custom_call_target="tpu_custom_call" | custom-call | flops 10000000000 | bytes 5489408 | tf_op jit(solution)/shard_map/pallas_call | solution.py:354
  38.7 0.0 collective-permute-done.1.refs_7_
  38.7 0.0 collective-permute-done.refs_6_
  38.8 3.1 %all-to-all-done.1 = f32[32,3,4,128]{3,2,1,0:T(4,128)S(1)} async-done(((f32[32,3,4,128]{3,2,1,0:T(4,128)}), f32[32,3,4,128]{3,2,1,0:T(4,128)S(1)}, u32[]{:S(2)}, u32[]{:S(2)}) %all-to-all-start.1) | async-done | bytes 196640 | tf_op jit(solution)/shard_map/all_to_all | solution.py:404
  41.8 3.7 %shard_map.106 = (f32[6,64,128]{2,1,0:T(8,128)}, f32[6,64,128]{2,1,0:T(8,128)}) custom-call(f32[6,64,128]{2,1,0:T(8,128)S(1)} %bitcast.15, bf16[64,256]{1,0:T(8,128)(2,1)S(1)} %get-tuple-element.15.refs_1_, f32[6,8,8,128]{3,2,1,0:T(8,128)S(1)} %get-tuple-element.16.refs_2_, f32[36,8,8,128]{3,2,1,0:T(8,128)S(1)} %get-tuple-element.17.refs_3_, ...), custom_call_target="tpu_custom_call" | custom-call | flops 3686400 | bytes 5636096 | tf_op jit(solution)/shard_map/pallas_call | solution.py:354
Async XLA Ops:
  0.6 31.3 %copy-start = (f32[6,6]{1,0:T(8,128)S(1)}, f32[6,6]{1,0:T(8,128)}, u32[]{:S(2)}) copy-start(f32[6,6]{1,0:T(8,128)} %refs_11_.1) | copy-start | bytes 436
  0.6 31.3 %copy-start.2 = (f32[6,6]{1,0:T(8,128)S(1)}, f32[6,6]{1,0:T(8,128)}, u32[]{:S(2)}) copy-start(f32[6,6]{1,0:T(8,128)} %refs_6_.1) | copy-start | bytes 436
  0.7 31.3 %copy-start.1 = (f32[6,6]{1,0:T(8,128)S(1)}, f32[6,6]{1,0:T(8,128)}, u32[]{:S(2)}) copy-start(f32[6,6]{1,0:T(8,128)} %refs_5_.1) | copy-start | bytes 436
  0.7 31.3 %copy-start.3 = (f32[6,6]{1,0:T(8,128)S(1)}, f32[6,6]{1,0:T(8,128)}, u32[]{:S(2)}) copy-start(f32[6,6]{1,0:T(8,128)} %refs_8_.1) | copy-start | bytes 436
  0.7 22.0 %all-to-all-start = ((f32[32,3,4,128]{3,2,1,0:T(4,128)}), f32[32,3,4,128]{3,2,1,0:T(4,128)S(1)}, u32[]{:S(2)}, u32[]{:S(2)}) async-start(f32[32,3,4,128]{3,2,1,0:T(4,128)} %bitcast.18), calls=%async_computation | async-start | bytes 393216 | tf_op jit(solution)/shard_map/all_to_all | solution.py:381
  11.0 27.7 %collective-permute-start.1 = (f32[6,2,8,128]{3,2,1,0:T(8,128)S(1)}, f32[6,2,8,128]{3,2,1,0:T(8,128)S(1)}, u32[]{:S(2)}, u32[]{:S(2)}) collective-permute-start(f32[6,2,8,128]{3,2,1,0:T(8,128)S(1)} %slice.3), channel_id=1, source_target_pairs={{1,2},{2,1},{3,4},{4,3},{5,6},{6,5},{7,8},{8,7},{9,10},{10,9},{11,... | collective-permute-start | bytes 147464 | tf_op jit(solution)/shard_map/ppermute | solution.py:389
  13.2 25.6 %collective-permute-start = (f32[6,2,8,128]{3,2,1,0:T(8,128)S(1)}, f32[6,2,8,128]{3,2,1,0:T(8,128)S(1)}, u32[]{:S(2)}, u32[]{:S(2)}) collective-permute-start(f32[6,2,8,128]{3,2,1,0:T(8,128)S(1)} %slice.3), channel_id=1, source_target_pairs={{0,1},{1,0},{2,3},{3,2},{4,5},{5,4},{6,7},{7,6},{8,9},{9,8},{10,11... | collective-permute-start | bytes 147464 | tf_op jit(solution)/shard_map/ppermute | solution.py:388
  23.7 18.2 %all-to-all-start.1 = ((f32[32,3,4,128]{3,2,1,0:T(4,128)}), f32[32,3,4,128]{3,2,1,0:T(4,128)S(1)}, u32[]{:S(2)}, u32[]{:S(2)}) async-start(f32[32,3,4,128]{3,2,1,0:T(4,128)} %bitcast.17), calls=%async_computation.1 | async-start | bytes 393216 | tf_op jit(solution)/shard_map/all_to_all | solution.py:404

commit v2 on v1

--- a/solution.py
+++ b/solution.py
@@ -385,7 +385,6 @@
     edges = state.reshape(variables, stations // NQ, NQ, radial)
     edges = edges[:, :: stations // NQ - 1]
     chips = lax.axis_size("space")
-    swap = lax.ppermute(edges, "space", [(i, i ^ 1) for i in range(chips)])
     other = lax.ppermute(edges, "space", [(i, ((i + 1) ^ 1) - 1) for i in range(1, chips - 1)])
     dma = pltpu.SemaphoreType.DMA
 
@@ -400,7 +399,8 @@
         2 * count * count * share * radial,
         [pltpu.VMEM((count * share, radial), jnp.float32), dma],
     )
-    timed, state = lax.optimization_barrier((timed, state))
+    timed, state, edges = lax.optimization_barrier((timed, state, edges))
+    swap = lax.ppermute(edges, "space", [(i, i ^ 1) for i in range(chips)])
     timed = lax.all_to_all(
         timed.reshape(count, share // 4, 4, radial), "inst", 0, 0, tiled=True
     ).reshape(variables, stations, radial)

time: 46 us -> 42.8 us (0.930)
  the two profiles are of different devices: /device:TPU:5 before, /device:TPU:7 now
where the time goes in v2:
time: 42.8 us; the launch traced here: 42.4 us
  starting transfers between devices  27.9 us (65%)
  Pallas kernels  11.4 us (27%)
  waiting for transfers between devices  1.37 us (3%)
  local copies, waits for them, and re-layouts  0.85 us (2%)
  between operations  0.77 us (2%)
    pallas_call x3, Pallas kernels, call(): pl.pallas_call(body, out_shape=outs, in_specs=[VMEM] * len(near) + [ANY]...  11.4 us
    all_to_all x1, starting transfers between devices, shards(): lax.all_to_all(state.reshape(count, share // 4, 4, radial), 'inst', 0, 0,...  9.5 us
    ppermute x1, starting transfers between devices, shards(): lax.ppermute(edges, 'space', [(i, (i + 1 ^ 1) - 1) for i in range(1, chip...  8.72 us
    all_to_all x1, starting transfers between devices, shards(): lax.all_to_all(timed.reshape(count, share // 4, 4, radial), 'inst', 0, 0,...  7.77 us
    ppermute x1, starting transfers between devices, shards(): swap = lax.ppermute(edges, 'space', [(i, i ^ 1) for i in range(chips)])  1.92 us
    all_to_all x1, waiting for transfers between devices, shards(): lax.all_to_all(timed.reshape(count, share // 4, 4, radial), 'inst', 0, 0,...  1.15 us
  transfers between devices with their start and end apart: 4, of which 2 were waited for; matrix products, arithmetic and copies ran while one was open for 2% of the time, Pallas kernels for 18%

profile of v2, /device:TPU:7, one launch (start us, length us, event | category | flops | bytes accessed | tf_op | source)
XLA Modules:
  0.0 42.4 jit_solution(272946972980870676)
XLA Ops:
  0.6 0.0 copy-start
  0.6 0.0 copy-start.2
  0.7 0.0 copy-start.1
  0.7 0.0 copy-start.3
  0.7 9.5 %all-to-all-start = ((f32[32,3,4,128]{3,2,1,0:T(4,128)}), f32[32,3,4,128]{3,2,1,0:T(4,128)S(1)}, u32[]{:S(2)}, u32[]{:S(2)}) async-start(f32[32,3,4,128]{3,2,1,0:T(4,128)} %bitcast.18), calls=%async_computation | async-start | bytes 393216 | tf_op jit(solution)/shard_map/all_to_all | solution.py:381
  10.2 0.8 %slice.3 = f32[6,2,8,128]{3,2,1,0:T(8,128)S(1)} slice(f32[6,8,8,128]{3,2,1,0:T(8,128)} %bitcast.19), slice={[0:6:1], [0:8:7], [0:8:1], [0:128:1]} | slice | bytes 98304 | tf_op jit(solution)/shard_map/slice | solution.py:386
  11.0 8.7 %collective-permute-start.1 = (f32[6,2,8,128]{3,2,1,0:T(8,128)S(1)}, f32[6,2,8,128]{3,2,1,0:T(8,128)S(1)}, u32[]{:S(2)}, u32[]{:S(2)}) collective-permute-start(f32[6,2,8,128]{3,2,1,0:T(8,128)S(1)} %slice.3), channel_id=1, source_target_pairs={{1,2},{2,1},{3,4},{4,3},{5,6},{6,5},{7,8},{8,7},{9,10},{10,9},{11,... | collective-permute-start | bytes 147464 | tf_op jit(solution)/shard_map/ppermute | solution.py:388
  19.8 0.1 multiply_subtract_fusion.spectral_ref
  19.9 0.2 all-to-all-done
  20.1 1.0 %shard_map.104 = f32[384,128]{1,0:T(8,128)} custom-call(f32[32,32]{1,0:T(8,128)S(1)} %multiply_subtract_fusion.spectral_ref, f32[384,128]{1,0:T(8,128)S(1)} %bitcast.16), custom_call_target="tpu_custom_call" | custom-call | flops 3145728 | bytes 397312 | tf_op jit(solution)/shard_map/pallas_call | solution.py:354
  21.0 7.8 %all-to-all-start.1 = ((f32[32,3,4,128]{3,2,1,0:T(4,128)}), f32[32,3,4,128]{3,2,1,0:T(4,128)S(1)}, u32[]{:S(2)}, u32[]{:S(2)}) async-start(f32[32,3,4,128]{3,2,1,0:T(4,128)} %bitcast.17), calls=%async_computation.1 | async-start | bytes 393216 | tf_op jit(solution)/shard_map/all_to_all | solution.py:404
  28.8 1.9 %collective-permute-start = (f32[6,2,8,128]{3,2,1,0:T(8,128)S(1)}, f32[6,2,8,128]{3,2,1,0:T(8,128)S(1)}, u32[]{:S(2)}, u32[]{:S(2)}) collective-permute-start(f32[6,2,8,128]{3,2,1,0:T(8,128)S(1)} %slice.3), channel_id=1, source_target_pairs={{0,1},{1,0},{2,3},{3,2},{4,5},{5,4},{6,7},{7,6},{8,9},{9,8},{10,11... | collective-permute-start | bytes 147464 | tf_op jit(solution)/shard_map/ppermute | solution.py:403
  30.7 0.0 copy-done
  30.8 0.0 copy-done.2
  30.8 0.0 copy-done.1
  30.8 0.0 copy-done.3
  30.8 6.8 %shard_map.105 = (f32[36,8,8,128]{3,2,1,0:T(8,128)S(1)}, f32[36,8,8,128]{3,2,1,0:T(8,128)S(1)}, f32[36,4,8,128]{3,2,1,0:T(8,128)S(1)}, f32[6,8,8,128]{3,2,1,0:T(...) custom-call(f32[36,8,128]{2,1,0:T(8,128)} %bitcast.24, ...), custom_call_target="tpu_custom_call" | custom-call | flops 10000000000 | bytes 5489408 | tf_op jit(solution)/shard_map/pallas_call | solution.py:354
  37.5 0.0 collective-permute-done.1.refs_7_
  37.6 0.0 collective-permute-done.refs_6_
  37.6 1.1 %all-to-all-done.1 = f32[32,3,4,128]{3,2,1,0:T(4,128)S(1)} async-done(((f32[32,3,4,128]{3,2,1,0:T(4,128)}), f32[32,3,4,128]{3,2,1,0:T(4,128)S(1)}, u32[]{:S(2)}, u32[]{:S(2)}) %all-to-all-start.1) | async-done | bytes 196640 | tf_op jit(solution)/shard_map/all_to_all | solution.py:404
  38.7 3.7 %shard_map.106 = (f32[6,64,128]{2,1,0:T(8,128)}, f32[6,64,128]{2,1,0:T(8,128)}) custom-call(f32[6,64,128]{2,1,0:T(8,128)S(1)} %bitcast.15, bf16[64,256]{1,0:T(8,128)(2,1)S(1)} %get-tuple-element.16.refs_1_, f32[6,8,8,128]{3,2,1,0:T(8,128)S(1)} %get-tuple-element.17.refs_2_, f32[36,8,8,128]{3,2,1,0:T(8,128)S(1)} %get-tuple-element.18.refs_3_, ...), custom_call_target="tpu_custom_call" | custom-call | flops 3686400 | bytes 5636096 | tf_op jit(solution)/shard_map/pallas_call | solution.py:354
Async XLA Ops:
  0.6 30.1 %copy-start = (f32[6,6]{1,0:T(8,128)S(1)}, f32[6,6]{1,0:T(8,128)}, u32[]{:S(2)}) copy-start(f32[6,6]{1,0:T(8,128)} %refs_11_.1) | copy-start | bytes 436
  0.6 30.1 %copy-start.2 = (f32[6,6]{1,0:T(8,128)S(1)}, f32[6,6]{1,0:T(8,128)}, u32[]{:S(2)}) copy-start(f32[6,6]{1,0:T(8,128)} %refs_6_.1) | copy-start | bytes 436
  0.7 30.1 %copy-start.1 = (f32[6,6]{1,0:T(8,128)S(1)}, f32[6,6]{1,0:T(8,128)}, u32[]{:S(2)}) copy-start(f32[6,6]{1,0:T(8,128)} %refs_5_.1) | copy-start | bytes 436
  0.7 30.1 %copy-start.3 = (f32[6,6]{1,0:T(8,128)S(1)}, f32[6,6]{1,0:T(8,128)}, u32[]{:S(2)}) copy-start(f32[6,6]{1,0:T(8,128)} %refs_8_.1) | copy-start | bytes 436
  0.7 19.4 %all-to-all-start = ((f32[32,3,4,128]{3,2,1,0:T(4,128)}), f32[32,3,4,128]{3,2,1,0:T(4,128)S(1)}, u32[]{:S(2)}, u32[]{:S(2)}) async-start(f32[32,3,4,128]{3,2,1,0:T(4,128)} %bitcast.18), calls=%async_computation | async-start | bytes 393216 | tf_op jit(solution)/shard_map/all_to_all | solution.py:381
  11.0 26.5 %collective-permute-start.1 = (f32[6,2,8,128]{3,2,1,0:T(8,128)S(1)}, f32[6,2,8,128]{3,2,1,0:T(8,128)S(1)}, u32[]{:S(2)}, u32[]{:S(2)}) collective-permute-start(f32[6,2,8,128]{3,2,1,0:T(8,128)S(1)} %slice.3), channel_id=1, source_target_pairs={{1,2},{2,1},{3,4},{4,3},{5,6},{6,5},{7,8},{8,7},{9,10},{10,9},{11,... | collective-permute-start | bytes 147464 | tf_op jit(solution)/shard_map/ppermute | solution.py:388
  21.0 17.7 %all-to-all-start.1 = ((f32[32,3,4,128]{3,2,1,0:T(4,128)}), f32[32,3,4,128]{3,2,1,0:T(4,128)S(1)}, u32[]{:S(2)}, u32[]{:S(2)}) async-start(f32[32,3,4,128]{3,2,1,0:T(4,128)} %bitcast.17), calls=%async_computation.1 | async-start | bytes 393216 | tf_op jit(solution)/shard_map/all_to_all | solution.py:404
  28.8 8.7 %collective-permute-start = (f32[6,2,8,128]{3,2,1,0:T(8,128)S(1)}, f32[6,2,8,128]{3,2,1,0:T(8,128)S(1)}, u32[]{:S(2)}, u32[]{:S(2)}) collective-permute-start(f32[6,2,8,128]{3,2,1,0:T(8,128)S(1)} %slice.3), channel_id=1, source_target_pairs={{0,1},{1,0},{2,3},{3,2},{4,5},{5,4},{6,7},{7,6},{8,9},{9,8},{10,11... | collective-permute-start | bytes 147464 | tf_op jit(solution)/shard_map/ppermute | solution.py:403

commit v3 on v2

--- a/solution.py
+++ b/solution.py
@@ -104,22 +104,12 @@
 
 
 def prepare_kernel(*refs):
-    table_hbm, offset_hbm, order_hbm, state_hbm, forcing_hbm = refs[:5]
-    lower_ref, upper_ref, axial_ref, radial_ref = refs[5:9]
-    factor_ref, a_ref, up_ref, local_ref, select_ref, b_out, down_out = refs[9:16]
-    table_ref, offset_ref, order_ref, state_ref, forcing_ref = refs[16:21]
-    b_ref, down_ref, turned_ref, sems, b_sem, down_sem = refs[21:]
-    copies = fetch(
-        [
-            (order_hbm, order_ref),
-            (offset_hbm, offset_ref),
-            (table_hbm, table_ref),
-            (state_hbm, state_ref),
-            (forcing_hbm, forcing_ref),
-        ],
-        sems,
-    )
-    for copy in copies[:3]:
+    factor_ref, a_ref, up_ref, local_ref, select_ref, slope_ref, b_out, down_out = refs[9:17]
+    table_ref, offset_ref, order_ref, lower_ref, upper_ref = refs[17:22]
+    axial_ref, radial_ref, state_ref, forcing_ref = refs[22:26]
+    b_ref, down_ref, turned_ref, sems, b_sem, down_sem = refs[26:]
+    copies = fetch(list(zip(refs[:9], refs[17:26])), sems)
+    for copy in copies[:5]:
         copy.wait()
     slot = lax.broadcasted_iota(jnp.int32, (LANES, LANES), 0)
     turned_ref[...] = (slot == order_ref[...]).astype(jnp.float32).T
@@ -184,8 +174,12 @@
             keep(ref, step, product(level, moved))
 
     stores += fetch([(down_ref, down_out)], down_sem)
-    for copy in copies[3:]:
+    for copy in copies[5:]:
         copy.wait()
+    for v in range(NV):
+        for w in range(NV):
+            row = jnp.full((1, LANES), 0.5 * axial_ref[v, w], jnp.float32)
+            slope_ref[v * NV + w : v * NV + w + 1] = row
     stations = state_ref.shape[1]
     row = lax.broadcasted_iota(jnp.int32, (stations, LANES), 0)
     state = [state_ref[v] for v in range(NV)]
@@ -270,25 +264,25 @@
 
 def solve_kernel(*refs):
     timed_ref, select_ref, local_ref, factor_ref, a_ref, up_ref, swap_ref, other_ref = refs[:8]
-    b_hbm, down_hbm, parity_ref, axial_ref, residual_hbm, correction_hbm = refs[8:14]
+    slope_ref, parity_ref, b_hbm, down_hbm, residual_hbm, correction_hbm = refs[8:14]
     joined_ref, b_ref, down_ref, residual_ref, correction_ref, lines_ref = refs[14:20]
     sems, residual_sems, correction_sems = refs[20:]
     loads = fetch([(b_hbm, b_ref), (down_hbm, down_ref)], sems)
-    even = parity_ref[0] == 0
-    high = [jnp.where(even, swap_ref[v, 0, :1], other_ref[v, 0, :1]) for v in range(NV)]
+    even = parity_ref[...] == 0.0
+    high = [jnp.where(even, swap_ref[v, :1], other_ref[v, :1]) for v in range(NV)]
     low = [
-        jnp.where(even, other_ref[v, 1, NQ - 1 :], swap_ref[v, 1, NQ - 1 :])
+        jnp.where(even, other_ref[v, 1:], swap_ref[v, 1:])
         for v in range(NV)
     ]
     row = lax.broadcasted_iota(jnp.int32, (NQ, LANES), 0)
     stations = timed_ref.shape[1]
     for v in range(NV):
-        before = sum_of([-0.5 * axial_ref[v, w] * low[w] for w in range(NV)]) - damping * low[v]
-        after = sum_of([0.5 * axial_ref[v, w] * high[w] for w in range(NV)]) - damping * high[v]
-        joined_ref[v, :NQ] = timed_ref[v, :NQ] + jnp.where(row == 0, before, 0.0)
+        before = -sum_of([slope_ref[v * NV + w : v * NV + w + 1] * low[w] for w in range(NV)])
+        after = sum_of([slope_ref[v * NV + w : v * NV + w + 1] * high[w] for w in range(NV)])
+        joined_ref[v, :NQ] = timed_ref[v, :NQ] + jnp.where(row == 0, before - damping * low[v], 0.0)
         joined_ref[v, NQ : stations - NQ] = timed_ref[v, NQ : stations - NQ]
         joined_ref[v, stations - NQ :] = timed_ref[v, stations - NQ :] + jnp.where(
-            row == NQ - 1, after, 0.0
+            row == NQ - 1, after - damping * high[v], 0.0
         )
     moved = picked(select_ref[...], doubled([joined_ref[v] for v in range(NV)]))
     own = []
@@ -334,7 +328,6 @@
         copy.wait()
 
 
-SMEM = pl.BlockSpec(memory_space=pltpu.SMEM)
 VMEM = pl.BlockSpec(memory_space=pltpu.VMEM)
 MIB = 2**20
 ANY = pl.BlockSpec(memory_space=pl.ANY)
@@ -345,7 +338,7 @@
     return jax.ShapeDtypeStruct(shape, jnp.float32)
 
 
-def call(body, near, far, small, near_outs, far_outs, limit, flops, scratch):
+def call(body, near, far, near_outs, far_outs, limit, flops, scratch):
     operands = [pltpu.with_memory_space_constraint(x, pltpu.VMEM) for x in near]
     operands += [pltpu.with_memory_space_constraint(x, pltpu.HBM) for x in far]
     outs = [pltpu.VMEM(x.shape, x.dtype) for x in near_outs]
@@ -354,12 +347,12 @@
     return pl.pallas_call(
         body,
         out_shape=outs,
-        in_specs=[VMEM] * len(near) + [ANY] * len(far) + [SMEM] * len(small),
+        in_specs=[VMEM] * len(near) + [ANY] * len(far),
         out_specs=[VMEM] * len(near_outs) + [ANY] * len(far_outs),
         scratch_shapes=list(scratch),
         compiler_params=pltpu.CompilerParams(vmem_limit_bytes=limit * MIB),
         cost_estimate=pl.CostEstimate(flops=flops, bytes_accessed=moved, transcendentals=0),
-    )(*operands, *small)
+    )(*operands)
 
 
 def shards(
@@ -382,8 +375,7 @@
         state.reshape(count, share // 4, 4, radial), "inst", 0, 0, tiled=True
     )
 
-    edges = state.reshape(variables, stations // NQ, NQ, radial)
-    edges = edges[:, :: stations // NQ - 1]
+    edges = state[:, :: stations - 1]
     chips = lax.axis_size("space")
     other = lax.ppermute(edges, "space", [(i, ((i + 1) ^ 1) - 1) for i in range(1, chips - 1)])
     dma = pltpu.SemaphoreType.DMA
@@ -391,7 +383,6 @@
     (timed,) = call(
         time_kernel,
         [spectral_matrix(count), gathered.reshape(count * share, radial)],
-        [],
         [],
         [],
         [f32(count * share, radial)],
@@ -418,26 +409,26 @@
         pivot_table.transpose(1, 2, 0, 3).reshape(NV * NV, KB, radial),
         block_offset.reshape(1, stations),
         line_perm.reshape(1, radial),
-        state,
-        forcing[0],
-    ]
-    factor, a_table, up_table, local, select, b_table, down_table = call(
+    ]
+    matrices = [lower_block, upper_block, axial_jac, radial_jac]
+    factor, a_table, up_table, local, select, slope, b_table, down_table = call(
         prepare_kernel,
         [],
-        inputs,
-        [lower_block, upper_block, axial_jac, radial_jac],
-        [coef, coef, level, lines, one_hot],
+        [*inputs, *matrices, state, forcing[0]],
+        [coef, coef, level, lines, one_hot, f32(NV * NV, radial)],
         [coef, level],
         16,
         PREP,
-        scratch(*inputs, coef, level, f32(LANES, LANES)) + [dma((5,)), dma((1,)), dma((1,))],
-    )
-    parity = (lax.axis_index("space") % 2).astype(jnp.int32).reshape(1)
+        scratch(*inputs)
+        + [pltpu.SMEM(x.shape, x.dtype) for x in matrices]
+        + scratch(state, forcing[0], coef, level, f32(LANES, LANES))
+        + [dma((9,)), dma((1,)), dma((1,))],
+    )
+    parity = jnp.full((1, radial), lax.axis_index("space") % 2, jnp.float32)
     residual, correction = call(
         solve_kernel,
-        [timed, select, local, factor, a_table, up_table, swap, other],
+        [timed, select, local, factor, a_table, up_table, swap, other, slope, parity],
         [b_table, down_table],
-        [parity, axial_jac],
         [],
         [cells, cells],
         16,

time: 42.8 us -> 42 us (0.981)
  Pallas kernels: 11.4 us -> 9.95 us
  waiting for transfers between devices: 1.37 us -> 2.02 us
    pallas_call x3, Pallas kernels: 11.4 us -> 9.95 us  [call(): pl.pallas_call(body, out_shape=outs, in_specs=[VMEM] * len(near) + [ANY]...]
    all_to_all x1, waiting for transfers between devices: 1.15 us -> 1.94 us  [shards(): lax.all_to_all(timed.reshape(count, share // 4, 4, radial), 'inst', 0, 0,...]
  transfers between devices with their start and end apart: 4 -> 4, of which waited for: 2 -> 2; matrix products, arithmetic and copies ran while one was open for 2% -> 3% of each run, Pallas kernels for 18% -> 17%
where the time goes in v3:
time: 42 us; the launch traced here: 41.7 us
  starting transfers between devices  27.9 us (66%)
  Pallas kernels  9.95 us (24%)
  waiting for transfers between devices  2.02 us (5%)
  local copies, waits for them, and re-layouts  0.98 us (2%)
  between operations  0.71 us (2%)
    pallas_call x3, Pallas kernels, call(): pl.pallas_call(body, out_shape=outs, in_specs=[VMEM] * len(near) + [ANY]...  9.95 us
    all_to_all x1, starting transfers between devices, shards(): lax.all_to_all(state.reshape(count, share // 4, 4, radial), 'inst', 0, 0,...  9.37 us
    ppermute x1, starting transfers between devices, shards(): lax.ppermute(edges, 'space', [(i, (i + 1 ^ 1) - 1) for i in range(1, chip...  8.72 us
    all_to_all x1, starting transfers between devices, shards(): lax.all_to_all(timed.reshape(count, share // 4, 4, radial), 'inst', 0, 0,...  7.92 us
    all_to_all x1, waiting for transfers between devices, shards(): lax.all_to_all(timed.reshape(count, share // 4, 4, radial), 'inst', 0, 0,...  1.94 us
    ppermute x1, starting transfers between devices, shards(): swap = lax.ppermute(edges, 'space', [(i, i ^ 1) for i in range(chips)])  1.92 us
    slice x1, local copies, waits for them, and re-layouts, shards(): edges = state[:, ::stations - 1]  0.98 us
  transfers between devices with their start and end apart: 4, of which 2 were waited for; matrix products, arithmetic and copies ran while one was open for 3% of the time, Pallas kernels for 17%

profile of v3, /device:TPU:7, one launch (start us, length us, event | category | flops | bytes accessed | tf_op | source)
XLA Modules:
  0.0 41.7 jit_solution(16594476151382090119)
XLA Ops:
  0.6 9.4 %all-to-all-start = ((f32[32,3,4,128]{3,2,1,0:T(4,128)}), f32[32,3,4,128]{3,2,1,0:T(4,128)S(1)}, u32[]{:S(2)}, u32[]{:S(2)}) async-start(f32[32,3,4,128]{3,2,1,0:T(4,128)} %bitcast.16), calls=%async_computation | async-start | bytes 393216 | tf_op jit(solution)/shard_map/all_to_all | solution.py:374
  10.0 1.0 %slice.3 = f32[6,2,128]{2,1,0:T(2,128)S(1)} slice(f32[6,64,128]{2,1,0:T(8,128)} %bitcast.17), slice={[0:6:1], [0:64:63], [0:128:1]} | slice | bytes 12288 | tf_op jit(solution)/shard_map/slice | solution.py:378
  11.0 8.7 %collective-permute-start.1 = (f32[6,2,128]{2,1,0:T(2,128)S(1)}, f32[6,2,128]{2,1,0:T(2,128)S(1)}, u32[]{:S(2)}, u32[]{:S(2)}) collective-permute-start(f32[6,2,128]{2,1,0:T(2,128)S(1)} %slice.3), channel_id=1, source_target_pairs={{1,2},{2,1},{3,4},{4,3},{5,6},{6,5},{7,8},{8,7},{9,10},{10,9},{11,... | collective-permute-start | bytes 18440 | tf_op jit(solution)/shard_map/ppermute | solution.py:380
  19.7 0.1 multiply_subtract_fusion.spectral_ref
  19.8 0.1 all-to-all-done
  19.9 1.0 %shard_map.104 = f32[384,128]{1,0:T(8,128)} custom-call(f32[32,32]{1,0:T(8,128)S(1)} %multiply_subtract_fusion.spectral_ref, f32[384,128]{1,0:T(8,128)S(1)} %bitcast.13), custom_call_target="tpu_custom_call" | custom-call | flops 3145728 | bytes 397312 | tf_op jit(solution)/shard_map/pallas_call | solution.py:347
  20.9 7.9 %all-to-all-start.1 = ((f32[32,3,4,128]{3,2,1,0:T(4,128)}), f32[32,3,4,128]{3,2,1,0:T(4,128)S(1)}, u32[]{:S(2)}, u32[]{:S(2)}) async-start(f32[32,3,4,128]{3,2,1,0:T(4,128)} %bitcast.15), calls=%async_computation.1 | async-start | bytes 393216 | tf_op jit(solution)/shard_map/all_to_all | solution.py:395
  28.8 1.9 %collective-permute-start = (f32[6,2,128]{2,1,0:T(2,128)S(1)}, f32[6,2,128]{2,1,0:T(2,128)S(1)}, u32[]{:S(2)}, u32[]{:S(2)}) collective-permute-start(f32[6,2,128]{2,1,0:T(2,128)S(1)} %slice.3), channel_id=1, source_target_pairs={{0,1},{1,0},{2,3},{3,2},{4,5},{5,4},{6,7},{7,6},{8,9},{9,8},{10,11... | collective-permute-start | bytes 18440 | tf_op jit(solution)/shard_map/ppermute | solution.py:394
  30.7 6.0 %shard_map.105 = (f32[36,8,8,128]{3,2,1,0:T(8,128)S(1)}, f32[36,8,8,128]{3,2,1,0:T(8,128)S(1)}, f32[36,4,8,128]{3,2,1,0:T(8,128)S(1)}, f32[6,8,8,128]{3,2,1,0:T(...) custom-call(f32[36,8,128]{2,1,0:T(8,128)} %bitcast.22, ...), custom_call_target="tpu_custom_call" | custom-call | flops 10000000000 | bytes 5508416 | tf_op jit(solution)/shard_map/pallas_call | solution.py:347
  36.7 0.0 collective-permute-done.1.refs_7_
  36.7 0.0 collective-permute-done.refs_6_
  36.7 1.9 %all-to-all-done.1 = f32[32,3,4,128]{3,2,1,0:T(4,128)S(1)} async-done(((f32[32,3,4,128]{3,2,1,0:T(4,128)}), f32[32,3,4,128]{3,2,1,0:T(4,128)S(1)}, u32[]{:S(2)}, u32[]{:S(2)}) %all-to-all-start.1) | async-done | bytes 196640 | tf_op jit(solution)/shard_map/all_to_all | solution.py:395
  38.7 3.0 %shard_map.106 = (f32[6,64,128]{2,1,0:T(8,128)}, f32[6,64,128]{2,1,0:T(8,128)}) custom-call(f32[6,64,128]{2,1,0:T(8,128)S(1)} %bitcast.14, bf16[64,256]{1,0:T(8,128)(2,1)S(1)} %get-tuple-element.17.refs_1_, f32[6,8,8,128]{3,2,1,0:T(8,128)S(1)} %get-tuple-element.18.refs_2_, f32[36,8,8,128]{3,2,1,0:T(8,128)S(1)} %get-tuple-element.19.refs_3_, ...), custom_call_target="tpu_custom_call" | custom-call | flops 3686400 | bytes 5569024 | tf_op jit(solution)/shard_map/pallas_call | solution.py:347
  (1 shorter events, 0.0 us)
Async XLA Ops:
  0.6 19.3 %all-to-all-start = ((f32[32,3,4,128]{3,2,1,0:T(4,128)}), f32[32,3,4,128]{3,2,1,0:T(4,128)S(1)}, u32[]{:S(2)}, u32[]{:S(2)}) async-start(f32[32,3,4,128]{3,2,1,0:T(4,128)} %bitcast.16), calls=%async_computation | async-start | bytes 393216 | tf_op jit(solution)/shard_map/all_to_all | solution.py:374
  11.0 25.7 %collective-permute-start.1 = (f32[6,2,128]{2,1,0:T(2,128)S(1)}, f32[6,2,128]{2,1,0:T(2,128)S(1)}, u32[]{:S(2)}, u32[]{:S(2)}) collective-permute-start(f32[6,2,128]{2,1,0:T(2,128)S(1)} %slice.3), channel_id=1, source_target_pairs={{1,2},{2,1},{3,4},{4,3},{5,6},{6,5},{7,8},{8,7},{9,10},{10,9},{11,... | collective-permute-start | bytes 18440 | tf_op jit(solution)/shard_map/ppermute | solution.py:380
  20.9 17.8 %all-to-all-start.1 = ((f32[32,3,4,128]{3,2,1,0:T(4,128)}), f32[32,3,4,128]{3,2,1,0:T(4,128)S(1)}, u32[]{:S(2)}, u32[]{:S(2)}) async-start(f32[32,3,4,128]{3,2,1,0:T(4,128)} %bitcast.15), calls=%async_computation.1 | async-start | bytes 393216 | tf_op jit(solution)/shard_map/all_to_all | solution.py:395
  28.8 7.9 %collective-permute-start = (f32[6,2,128]{2,1,0:T(2,128)S(1)}, f32[6,2,128]{2,1,0:T(2,128)S(1)}, u32[]{:S(2)}, u32[]{:S(2)}) collective-permute-start(f32[6,2,128]{2,1,0:T(2,128)S(1)} %slice.3), channel_id=1, source_target_pairs={{0,1},{1,0},{2,3},{3,2},{4,5},{5,4},{6,7},{7,6},{8,9},{9,8},{10,11... | collective-permute-start | bytes 18440 | tf_op jit(solution)/shard_map/ppermute | solution.py:394

commit v4 on v3

--- a/solution.py
+++ b/solution.py
@@ -101,6 +101,16 @@
     for copy in copies:
         copy.start()
     return copies
+
+
+def edges_kernel(state_hbm, edges_ref, sems):
+    last = state_hbm.shape[1] - 1
+    copies = fetch(
+        [(state_hbm.at[:, pl.ds(i * last, 1)], edges_ref.at[:, pl.ds(i, 1)]) for i in range(2)],
+        sems,
+    )
+    for copy in copies:
+        copy.wait()
 
 
 def prepare_kernel(*refs):
@@ -310,11 +320,11 @@
     for t in range(NS):
         carry = [x + y for x, y in zip(own[t], applied(a_ref, (t,), carry))]
         sweep.append(carry)
-    for copy in loads:
-        copy.wait()
+    loads[0].wait()
     ends = sweep[NS - 1]
     for t in reversed(range(NS - 1)):
         ends = [x + y for x, y in zip(sweep[t], applied(b_ref, (t,), ends))]
+    loads[1].wait()
     for step in range(LEVELS):
         more = applied(down_ref, (step,), [shift_chunks(x, -(2**step)) for x in ends])
         ends = [x + y for x, y in zip(ends, more)]
@@ -375,10 +385,19 @@
         state.reshape(count, share // 4, 4, radial), "inst", 0, 0, tiled=True
     )
 
-    edges = state[:, :: stations - 1]
+    dma = pltpu.SemaphoreType.DMA
+    (edges,) = call(
+        edges_kernel,
+        [],
+        [state],
+        [f32(variables, 2, radial)],
+        [],
+        4,
+        1,
+        [dma((2,))],
+    )
     chips = lax.axis_size("space")
     other = lax.ppermute(edges, "space", [(i, ((i + 1) ^ 1) - 1) for i in range(1, chips - 1)])
-    dma = pltpu.SemaphoreType.DMA
 
     (timed,) = call(
         time_kernel,

time: 42 us -> 41.7 us (level)
  local copies, waits for them, and re-layouts: 0.98 us -> 0.01 us
  Pallas kernels: 9.95 us -> 10.6 us
    slice x1 -> x0, local copies, waits for them, and re-layouts: 0.98 us -> none  [shards(): edges = state[:, ::stations - 1]]
    pallas_call x3 -> x4, Pallas kernels: 9.95 us -> 10.6 us  [call(): pl.pallas_call(body, out_shape=outs, in_specs=[VMEM] * len(near) + [ANY]...]
  transfers between devices with their start and end apart: 4 -> 4, of which waited for: 2 -> 2; matrix products, arithmetic and copies ran while one was open for 3% -> 0% of each run, Pallas kernels for 17% -> 19%
where the time goes in v4:
time: 41.7 us; the launch traced here: 41.4 us
  starting transfers between devices  27.7 us (66%)
  Pallas kernels  10.6 us (25%)
  waiting for transfers between devices  2.23 us (5%)
  between operations  0.72 us (2%)
    pallas_call x4, Pallas kernels, call(): pl.pallas_call(body, out_shape=outs, in_specs=[VMEM] * len(near) + [ANY]...  10.6 us
    all_to_all x1, starting transfers between devices, shards(): lax.all_to_all(state.reshape(count, share // 4, 4, radial), 'inst', 0, 0,...  9.37 us
    ppermute x1, starting transfers between devices, shards(): lax.ppermute(edges, 'space', [(i, (i + 1 ^ 1) - 1) for i in range(1, chip...  8.73 us
    all_to_all x1, starting transfers between devices, shards(): lax.all_to_all(timed.reshape(count, share // 4, 4, radial), 'inst', 0, 0,...  7.69 us
    ppermute x1, starting transfers between devices, shards(): swap = lax.ppermute(edges, 'space', [(i, i ^ 1) for i in range(chips)])  1.92 us
    all_to_all x1, waiting for transfers between devices, shards(): lax.all_to_all(timed.reshape(count, share // 4, 4, radial), 'inst', 0, 0,...  1.91 us
  transfers between devices with their start and end apart: 4, of which 2 were waited for; matrix products, arithmetic and copies ran while one was open for 0% of the time, Pallas kernels for 19%

profile of v4, /device:TPU:7, one launch (start us, length us, event | category | flops | bytes accessed | tf_op | source)
XLA Modules:
  0.0 41.4 jit_solution(1901348286338271056)
XLA Ops:
  0.6 9.4 %all-to-all-start = ((f32[32,3,4,128]{3,2,1,0:T(4,128)}), f32[32,3,4,128]{3,2,1,0:T(4,128)S(1)}, u32[]{:S(2)}, u32[]{:S(2)}) async-start(f32[32,3,4,128]{3,2,1,0:T(4,128)} %bitcast.15), calls=%async_computation | async-start | bytes 393216 | tf_op jit(solution)/shard_map/all_to_all | solution.py:384
  10.0 0.7 %shard_map.105 = f32[6,2,128]{2,1,0:T(2,128)S(1)} custom-call(f32[6,64,128]{2,1,0:T(8,128)} %bitcast.16), custom_call_target="tpu_custom_call" | custom-call | flops 1 | bytes 202752 | tf_op jit(solution)/shard_map/pallas_call | solution.py:357
  10.7 8.7 %collective-permute-start.1 = (f32[6,2,128]{2,1,0:T(2,128)S(1)}, f32[6,2,128]{2,1,0:T(2,128)S(1)}, u32[]{:S(2)}, u32[]{:S(2)}) collective-permute-start(f32[6,2,128]{2,1,0:T(2,128)S(1)} %shard_map.105), channel_id=1, source_target_pairs={{1,2},{2,1},{3,4},{4,3},{5,6},{6,5},{7,8},{8,7},{9,10},{10,9},{11,... | collective-permute-start | bytes 18440 | tf_op jit(solution)/shard_map/ppermute | solution.py:400
  19.5 0.1 multiply_subtract_fusion.spectral_ref
  19.6 0.3 all-to-all-done
  19.9 1.0 %shard_map.104 = f32[384,128]{1,0:T(8,128)} custom-call(f32[32,32]{1,0:T(8,128)S(1)} %multiply_subtract_fusion.spectral_ref, f32[384,128]{1,0:T(8,128)S(1)} %bitcast.13), custom_call_target="tpu_custom_call" | custom-call | flops 3145728 | bytes 397312 | tf_op jit(solution)/shard_map/pallas_call | solution.py:357
  20.9 7.7 %all-to-all-start.1 = ((f32[32,3,4,128]{3,2,1,0:T(4,128)}), f32[32,3,4,128]{3,2,1,0:T(4,128)S(1)}, u32[]{:S(2)}, u32[]{:S(2)}) async-start(f32[32,3,4,128]{3,2,1,0:T(4,128)} %bitcast.18), calls=%async_computation.1 | async-start | bytes 393216 | tf_op jit(solution)/shard_map/all_to_all | solution.py:414
  28.6 1.9 %collective-permute-start = (f32[6,2,128]{2,1,0:T(2,128)S(1)}, f32[6,2,128]{2,1,0:T(2,128)S(1)}, u32[]{:S(2)}, u32[]{:S(2)}) collective-permute-start(f32[6,2,128]{2,1,0:T(2,128)S(1)} %shard_map.105), channel_id=1, source_target_pairs={{0,1},{1,0},{2,3},{3,2},{4,5},{5,4},{6,7},{7,6},{8,9},{9,8},{10,11... | collective-permute-start | bytes 18440 | tf_op jit(solution)/shard_map/ppermute | solution.py:413
  30.5 6.0 %shard_map.106 = (f32[36,8,8,128]{3,2,1,0:T(8,128)S(1)}, f32[36,8,8,128]{3,2,1,0:T(8,128)S(1)}, f32[36,4,8,128]{3,2,1,0:T(8,128)S(1)}, f32[6,8,8,128]{3,2,1,0:T(...) custom-call(f32[36,8,128]{2,1,0:T(8,128)} %bitcast.22, ...), custom_call_target="tpu_custom_call" | custom-call | flops 10000000000 | bytes 5508416 | tf_op jit(solution)/shard_map/pallas_call | solution.py:357
  36.5 0.0 collective-permute-done.1.refs_7_
  36.5 0.0 collective-permute-done.refs_6_
  36.5 1.9 %all-to-all-done.1 = f32[32,3,4,128]{3,2,1,0:T(4,128)S(1)} async-done(((f32[32,3,4,128]{3,2,1,0:T(4,128)}), f32[32,3,4,128]{3,2,1,0:T(4,128)S(1)}, u32[]{:S(2)}, u32[]{:S(2)}) %all-to-all-start.1) | async-done | bytes 196640 | tf_op jit(solution)/shard_map/all_to_all | solution.py:414
  38.5 2.9 %shard_map.107 = (f32[6,64,128]{2,1,0:T(8,128)}, f32[6,64,128]{2,1,0:T(8,128)}) custom-call(f32[6,64,128]{2,1,0:T(8,128)S(1)} %bitcast.14, bf16[64,256]{1,0:T(8,128)(2,1)S(1)} %get-tuple-element.17.refs_1_, f32[6,8,8,128]{3,2,1,0:T(8,128)S(1)} %get-tuple-element.18.refs_2_, f32[36,8,8,128]{3,2,1,0:T(8,128)S(1)} %get-tuple-element.19.refs_3_, ...), custom_call_target="tpu_custom_call" | custom-call | flops 3686400 | bytes 5569024 | tf_op jit(solution)/shard_map/pallas_call | solution.py:357
  (1 shorter events, 0.0 us)
Async XLA Ops:
  0.6 19.3 %all-to-all-start = ((f32[32,3,4,128]{3,2,1,0:T(4,128)}), f32[32,3,4,128]{3,2,1,0:T(4,128)S(1)}, u32[]{:S(2)}, u32[]{:S(2)}) async-start(f32[32,3,4,128]{3,2,1,0:T(4,128)} %bitcast.15), calls=%async_computation | async-start | bytes 393216 | tf_op jit(solution)/shard_map/all_to_all | solution.py:384
  10.7 25.8 %collective-permute-start.1 = (f32[6,2,128]{2,1,0:T(2,128)S(1)}, f32[6,2,128]{2,1,0:T(2,128)S(1)}, u32[]{:S(2)}, u32[]{:S(2)}) collective-permute-start(f32[6,2,128]{2,1,0:T(2,128)S(1)} %shard_map.105), channel_id=1, source_target_pairs={{1,2},{2,1},{3,4},{4,3},{5,6},{6,5},{7,8},{8,7},{9,10},{10,9},{11,... | collective-permute-start | bytes 18440 | tf_op jit(solution)/shard_map/ppermute | solution.py:400
  20.9 17.6 %all-to-all-start.1 = ((f32[32,3,4,128]{3,2,1,0:T(4,128)}), f32[32,3,4,128]{3,2,1,0:T(4,128)S(1)}, u32[]{:S(2)}, u32[]{:S(2)}) async-start(f32[32,3,4,128]{3,2,1,0:T(4,128)} %bitcast.18), calls=%async_computation.1 | async-start | bytes 393216 | tf_op jit(solution)/shard_map/all_to_all | solution.py:414
  28.6 8.0 %collective-permute-start = (f32[6,2,128]{2,1,0:T(2,128)S(1)}, f32[6,2,128]{2,1,0:T(2,128)S(1)}, u32[]{:S(2)}, u32[]{:S(2)}) collective-permute-start(f32[6,2,128]{2,1,0:T(2,128)S(1)} %shard_map.105), channel_id=1, source_target_pairs={{0,1},{1,0},{2,3},{3,2},{4,5},{5,4},{6,7},{7,6},{8,9},{9,8},{10,11... | collective-permute-start | bytes 18440 | tf_op jit(solution)/shard_map/ppermute | solution.py:413

commit v5 on v4

--- a/solution.py
+++ b/solution.py
@@ -1,5 +1,6 @@
 import jax
 import jax.numpy as jnp
+import numpy as np
 from jax import lax
 from jax.experimental import pallas as pl
 from jax.experimental.pallas import tpu as pltpu
@@ -18,19 +19,21 @@
 LEVELS = 4
 
 
-def spectral_matrix(count):
-    row_index = lax.broadcasted_iota(jnp.int32, (count, count), 0)
-    col_index = lax.broadcasted_iota(jnp.int32, (count, count), 1)
-    distance = row_index - col_index
-    parity = (1 - 2 * jnp.mod(distance, 2)).astype(jnp.float32)
-    phase_angle = jnp.pi * distance.astype(jnp.float32) / count
-    diagonal_mask = distance == 0
-    sine_value = jnp.where(diagonal_mask, 1.0, jnp.sin(phase_angle))
-    first_order = jnp.where(diagonal_mask, 0.0, 0.5 * parity * jnp.cos(phase_angle) / sine_value)
-    second_order = jnp.where(
-        diagonal_mask, -(count * count + 2) / 12.0, -0.5 * parity / (sine_value * sine_value)
-    )
-    return frequency * first_order - viscosity * second_order
+def spectral_weight(count):
+    distance = np.arange(count)[:, None] - np.arange(count)[None]
+    parity = 1.0 - 2.0 * (distance % 2)
+    angle = np.pi * distance / count
+    diagonal = distance == 0
+    sine = np.where(diagonal, 1.0, np.sin(angle))
+    first = np.where(diagonal, 0.0, 0.5 * parity * np.cos(angle) / sine)
+    second = np.where(diagonal, -(count * count + 2) / 12.0, -0.5 * parity / (sine * sine))
+    rest = (frequency * first - viscosity * second).astype(np.float32)
+    parts = []
+    for _ in range(3):
+        parts.append(rest.astype(jnp.bfloat16))
+        rest = rest - parts[-1].astype(np.float32)
+    high, middle, low = parts
+    return np.concatenate([high, high, middle, high, low, middle], axis=1)
 
 
 def shift_chunks(tile, amount):
@@ -103,13 +106,10 @@
     return copies
 
 
-def edges_kernel(state_hbm, edges_ref, sems):
+def edges_kernel(state_hbm, weight_hbm, edges_ref, weight_ref, sems):
     last = state_hbm.shape[1] - 1
-    copies = fetch(
-        [(state_hbm.at[:, pl.ds(i * last, 1)], edges_ref.at[:, pl.ds(i, 1)]) for i in range(2)],
-        sems,
-    )
-    for copy in copies:
+    pairs = [(state_hbm.at[:, pl.ds(i * last, 1)], edges_ref.at[:, pl.ds(i, 1)]) for i in range(2)]
+    for copy in fetch([*pairs, (weight_hbm, weight_ref)], sems):
         copy.wait()
 
 
@@ -176,7 +176,8 @@
         keep(down_ref, 0, product(load(b_ref, NS - 1 - t), load(down_ref, 0)))
         return carry
 
-    lax.fori_loop(1, NS, extend, 0)
+    for t in range(1, NS):
+        extend(t, 0)
     for ref, sign in ((up_ref, 1), (down_ref, -1)):
         for step in range(1, LEVELS):
             level = load(ref, step - 1)
@@ -231,17 +232,15 @@
         copy.wait()
 
 
-def time_kernel(spectral_ref, state_ref, timed_hbm, timed_ref, sem):
-    count = spectral_ref.shape[0]
+def time_kernel(weight_ref, state_ref, timed_hbm, timed_ref, sem):
+    count = weight_ref.shape[0]
     rows = state_ref.shape[0] // count
-    high, middle, low = split(spectral_ref[...])
-    weight = jnp.concatenate([high, high, middle, high, low, middle], axis=1)
     stacked = jnp.concatenate(
         [state_ref[pl.ds(row, count, stride=rows), :] for row in range(rows)], axis=1
     )
     high, middle, low = split(stacked)
     result = jnp.dot(
-        weight,
+        weight_ref[...],
         jnp.concatenate([high, middle, high, low, high, middle], axis=0),
         preferred_element_type=jnp.float32,
     )
@@ -252,31 +251,25 @@
     copy.wait()
 
 
-def from_lines(lines_ref, out_ref, out_hbm, sems):
+def from_lines(lines_ref, out_ref, pair):
     lane = lax.broadcasted_iota(jnp.int32, (LANES // 2, LANES), 1)
     half = LANES // 2
-    copies = []
-    for pair in range(NV // 2):
-        rows = [
-            lines_ref[2 * pair + p, pl.ds(sub, NS, stride=NQ), :]
-            for p in range(2)
-            for sub in range(NQ)
-        ]
-        turned = jnp.concatenate(rows, axis=0).T
-        top, bottom = turned[:half], turned[half:]
-        out_ref[2 * pair] = jnp.where(lane < half, top, pltpu.roll(bottom, half, 1))
-        out_ref[2 * pair + 1] = jnp.where(lane < half, pltpu.roll(top, half, 1), bottom)
-        both = pl.ds(2 * pair, 2)
-        copies.append(pltpu.make_async_copy(out_ref.at[both], out_hbm.at[both], sems.at[pair]))
-        copies[-1].start()
-    return copies
+    rows = [
+        lines_ref[2 * pair + p, pl.ds(sub, NS, stride=NQ), :]
+        for p in range(2)
+        for sub in range(NQ)
+    ]
+    turned = jnp.concatenate(rows, axis=0).T
+    top, bottom = turned[:half], turned[half:]
+    out_ref[2 * pair] = jnp.where(lane < half, top, pltpu.roll(bottom, half, 1))
+    out_ref[2 * pair + 1] = jnp.where(lane < half, pltpu.roll(top, half, 1), bottom)
 
 
 def solve_kernel(*refs):
     timed_ref, select_ref, local_ref, factor_ref, a_ref, up_ref, swap_ref, other_ref = refs[:8]
     slope_ref, parity_ref, b_hbm, down_hbm, residual_hbm, correction_hbm = refs[8:14]
     joined_ref, b_ref, down_ref, residual_ref, correction_ref, lines_ref = refs[14:20]
-    sems, residual_sems, correction_sems = refs[20:]
+    sems, residual_sem, correction_sems = refs[20:]
     loads = fetch([(b_hbm, b_ref), (down_hbm, down_ref)], sems)
     even = parity_ref[...] == 0.0
     high = [jnp.where(even, swap_ref[v, :1], other_ref[v, :1]) for v in range(NV)]
@@ -310,7 +303,8 @@
         if t > 0:
             value = [x + y for x, y in zip(value, applied(a_ref, (t,), ends))]
         ends = value
-    copies = from_lines(lines_ref, residual_ref, residual_hbm, residual_sems)
+    for pair in range(NV // 2):
+        from_lines(lines_ref, residual_ref, pair)
 
     for step in range(LEVELS):
         more = applied(up_ref, (step,), [shift_chunks(x, 2**step) for x in ends])
@@ -320,6 +314,7 @@
     for t in range(NS):
         carry = [x + y for x, y in zip(own[t], applied(a_ref, (t,), carry))]
         sweep.append(carry)
+    copies = fetch([(residual_ref, residual_hbm)], residual_sem)
     loads[0].wait()
     ends = sweep[NS - 1]
     for t in reversed(range(NS - 1)):
@@ -333,7 +328,15 @@
         carry = [x + y for x, y in zip(sweep[t], applied(b_ref, (t,), carry))]
         for v in range(NV):
             lines_ref[v, t * NQ : (t + 1) * NQ] = carry[v]
-    copies += from_lines(lines_ref, correction_ref, correction_hbm, correction_sems)
+    for pair in range(NV // 2):
+        from_lines(lines_ref, correction_ref, pair)
+        both = pl.ds(2 * pair, 2)
+        copies.append(
+            pltpu.make_async_copy(
+                correction_ref.at[both], correction_hbm.at[both], correction_sems.at[pair]
+            )
+        )
+        copies[-1].start()
     for copy in copies:
         copy.wait()
 
@@ -386,22 +389,23 @@
     )
 
     dma = pltpu.SemaphoreType.DMA
-    (edges,) = call(
+    weight = jnp.asarray(spectral_weight(count))
+    edges, weight = call(
         edges_kernel,
         [],
-        [state],
-        [f32(variables, 2, radial)],
+        [state, weight],
+        [f32(variables, 2, radial), weight],
         [],
         4,
         1,
-        [dma((2,))],
+        [dma((3,))],
     )
     chips = lax.axis_size("space")
     other = lax.ppermute(edges, "space", [(i, ((i + 1) ^ 1) - 1) for i in range(1, chips - 1)])
 
     (timed,) = call(
         time_kernel,
-        [spectral_matrix(count), gathered.reshape(count * share, radial)],
+        [weight, gathered.reshape(count * share, radial)],
         [],
         [],
         [f32(count * share, radial)],
@@ -456,7 +460,7 @@
         + [
             pltpu.VMEM((NV, NS * NQ, LANES), jnp.float32),
             dma((2,)),
-            dma((NV // 2,)),
+            dma((1,)),
             dma((NV // 2,)),
         ],
     )

time: 41.7 us -> 41.7 us (level)
  waiting for transfers between devices: 2.23 us -> 3.15 us
  Pallas kernels: 10.6 us -> 9.73 us
    pallas_call x4, Pallas kernels: 10.6 us -> 9.73 us  [call(): pl.pallas_call(body, out_shape=outs, in_specs=[VMEM] * len(near) + [ANY]...]
    all_to_all x1, waiting for transfers between devices: 1.91 us -> 2.79 us  [shards(): lax.all_to_all(timed.reshape(count, share // 4, 4, radial), 'inst', 0, 0,...]
  transfers between devices with their start and end apart: 4 -> 4, of which waited for: 2 -> 2; matrix products, arithmetic and copies ran while one was open for 0% -> 0% of each run, Pallas kernels for 19% -> 17%
where the time goes in v5:
time: 41.7 us; the launch traced here: 41.3 us
  starting transfers between devices  27.7 us (66%)
  Pallas kernels  9.73 us (23%)
  waiting for transfers between devices  3.15 us (8%)
  between operations  0.71 us (2%)
    pallas_call x4, Pallas kernels, call(): pl.pallas_call(body, out_shape=outs, in_specs=[VMEM] * len(near) + [ANY]...  9.73 us
    all_to_all x1, starting transfers between devices, shards(): lax.all_to_all(state.reshape(count, share // 4, 4, radial), 'inst', 0, 0,...  9.37 us
    ppermute x1, starting transfers between devices, shards(): lax.ppermute(edges, 'space', [(i, (i + 1 ^ 1) - 1) for i in range(1, chip...  8.73 us
    all_to_all x1, starting transfers between devices, shards(): lax.all_to_all(timed.reshape(count, share // 4, 4, radial), 'inst', 0, 0,...  7.63 us
    all_to_all x1, waiting for transfers between devices, shards(): lax.all_to_all(timed.reshape(count, share // 4, 4, radial), 'inst', 0, 0,...  2.79 us
    ppermute x1, starting transfers between devices, shards(): swap = lax.ppermute(edges, 'space', [(i, i ^ 1) for i in range(chips)])  1.92 us
  transfers between devices with their start and end apart: 4, of which 2 were waited for; matrix products, arithmetic and copies ran while one was open for 0% of the time, Pallas kernels for 17%

profile of v5, /device:TPU:7, one launch (start us, length us, event | category | flops | bytes accessed | tf_op | source)
XLA Modules:
  0.0 41.3 jit_solution(18304272171209816745)
XLA Ops:
  0.6 9.4 %all-to-all-start = ((f32[32,3,4,128]{3,2,1,0:T(4,128)}), f32[32,3,4,128]{3,2,1,0:T(4,128)S(1)}, u32[]{:S(2)}, u32[]{:S(2)}) async-start(f32[32,3,4,128]{3,2,1,0:T(4,128)} %bitcast.15), calls=%async_computation | async-start | bytes 393216 | tf_op jit(solution)/shard_map/all_to_all | solution.py:387
  10.0 0.8 %shard_map.113 = (f32[6,2,128]{2,1,0:T(2,128)S(1)}, bf16[32,192]{1,0:T(8,128)(2,1)S(1)}) custom-call(f32[6,64,128]{2,1,0:T(8,128)} %bitcast.16, bf16[32,192]{1,0:T(8,128)(2,1)} %constant.19.clone.weight_hbm), custom_call_target="tpu_custom_call" | custom-call | flops 1 | bytes 227328 | tf_op jit(solution)/shard_map/pallas_call | solution.py:360
  10.8 8.7 %collective-permute-start.1 = (f32[6,2,128]{2,1,0:T(2,128)S(1)}, f32[6,2,128]{2,1,0:T(2,128)S(1)}, u32[]{:S(2)}, u32[]{:S(2)}) collective-permute-start(f32[6,2,128]{2,1,0:T(2,128)S(1)} %get-tuple-element.26), channel_id=1, source_target_pairs={{1,2},{2,1},{3,4},{4,3},{5,6},{6,5},{7,8},{8,7},{9,10},{10,9},{11,... | collective-permute-start | bytes 18440 | tf_op jit(solution)/shard_map/ppermute | solution.py:404
  19.5 0.4 all-to-all-done
  19.9 0.9 %shard_map.114 = f32[384,128]{1,0:T(8,128)} custom-call(bf16[32,192]{1,0:T(8,128)(2,1)S(1)} %get-tuple-element.17.weight_ref, f32[384,128]{1,0:T(8,128)S(1)} %bitcast.13), custom_call_target="tpu_custom_call" | custom-call | flops 3145728 | bytes 405504 | tf_op jit(solution)/shard_map/pallas_call | solution.py:360
  20.8 7.6 %all-to-all-start.1 = ((f32[32,3,4,128]{3,2,1,0:T(4,128)}), f32[32,3,4,128]{3,2,1,0:T(4,128)S(1)}, u32[]{:S(2)}, u32[]{:S(2)}) async-start(f32[32,3,4,128]{3,2,1,0:T(4,128)} %bitcast.18), calls=%async_computation.1 | async-start | bytes 393216 | tf_op jit(solution)/shard_map/all_to_all | solution.py:418
  28.5 1.9 %collective-permute-start = (f32[6,2,128]{2,1,0:T(2,128)S(1)}, f32[6,2,128]{2,1,0:T(2,128)S(1)}, u32[]{:S(2)}, u32[]{:S(2)}) collective-permute-start(f32[6,2,128]{2,1,0:T(2,128)S(1)} %get-tuple-element.26), channel_id=1, source_target_pairs={{0,1},{1,0},{2,3},{3,2},{4,5},{5,4},{6,7},{7,6},{8,9},{9,8},{10,11... | collective-permute-start | bytes 18440 | tf_op jit(solution)/shard_map/ppermute | solution.py:417
  30.4 5.1 %shard_map.115 = (f32[36,8,8,128]{3,2,1,0:T(8,128)S(1)}, f32[36,8,8,128]{3,2,1,0:T(8,128)S(1)}, f32[36,4,8,128]{3,2,1,0:T(8,128)S(1)}, f32[6,8,8,128]{3,2,1,0:T(...) custom-call(f32[36,8,128]{2,1,0:T(8,128)} %bitcast.22, ...), custom_call_target="tpu_custom_call" | custom-call | flops 10000000000 | bytes 5508416 | tf_op jit(solution)/shard_map/pallas_call | solution.py:360
  35.5 0.0 collective-permute-done.1.refs_7_
  35.6 0.0 collective-permute-done.refs_6_
  35.6 2.8 %all-to-all-done.1 = f32[32,3,4,128]{3,2,1,0:T(4,128)S(1)} async-done(((f32[32,3,4,128]{3,2,1,0:T(4,128)}), f32[32,3,4,128]{3,2,1,0:T(4,128)S(1)}, u32[]{:S(2)}, u32[]{:S(2)}) %all-to-all-start.1) | async-done | bytes 196640 | tf_op jit(solution)/shard_map/all_to_all | solution.py:418
  38.4 2.9 %shard_map.116 = (f32[6,64,128]{2,1,0:T(8,128)}, f32[6,64,128]{2,1,0:T(8,128)}) custom-call(f32[6,64,128]{2,1,0:T(8,128)S(1)} %bitcast.14, bf16[64,256]{1,0:T(8,128)(2,1)S(1)} %get-tuple-element.21.refs_1_, f32[6,8,8,128]{3,2,1,0:T(8,128)S(1)} %get-tuple-element.22.refs_2_, f32[36,8,8,128]{3,2,1,0:T(8,128)S(1)} %get-tuple-element.23.refs_3_, ...), custom_call_target="tpu_custom_call" | custom-call | flops 3686400 | bytes 5569024 | tf_op jit(solution)/shard_map/pallas_call | solution.py:360
  (1 shorter events, 0.0 us)
Async XLA Ops:
  0.6 19.3 %all-to-all-start = ((f32[32,3,4,128]{3,2,1,0:T(4,128)}), f32[32,3,4,128]{3,2,1,0:T(4,128)S(1)}, u32[]{:S(2)}, u32[]{:S(2)}) async-start(f32[32,3,4,128]{3,2,1,0:T(4,128)} %bitcast.15), calls=%async_computation | async-start | bytes 393216 | tf_op jit(solution)/shard_map/all_to_all | solution.py:387
  10.8 24.7 %collective-permute-start.1 = (f32[6,2,128]{2,1,0:T(2,128)S(1)}, f32[6,2,128]{2,1,0:T(2,128)S(1)}, u32[]{:S(2)}, u32[]{:S(2)}) collective-permute-start(f32[6,2,128]{2,1,0:T(2,128)S(1)} %get-tuple-element.26), channel_id=1, source_target_pairs={{1,2},{2,1},{3,4},{4,3},{5,6},{6,5},{7,8},{8,7},{9,10},{10,9},{11,... | collective-permute-start | bytes 18440 | tf_op jit(solution)/shard_map/ppermute | solution.py:404
  20.8 17.5 %all-to-all-start.1 = ((f32[32,3,4,128]{3,2,1,0:T(4,128)}), f32[32,3,4,128]{3,2,1,0:T(4,128)S(1)}, u32[]{:S(2)}, u32[]{:S(2)}) async-start(f32[32,3,4,128]{3,2,1,0:T(4,128)} %bitcast.18), calls=%async_computation.1 | async-start | bytes 393216 | tf_op jit(solution)/shard_map/all_to_all | solution.py:418
  28.5 7.1 %collective-permute-start = (f32[6,2,128]{2,1,0:T(2,128)S(1)}, f32[6,2,128]{2,1,0:T(2,128)S(1)}, u32[]{:S(2)}, u32[]{:S(2)}) collective-permute-start(f32[6,2,128]{2,1,0:T(2,128)S(1)} %get-tuple-element.26), channel_id=1, source_target_pairs={{0,1},{1,0},{2,3},{3,2},{4,5},{5,4},{6,7},{7,6},{8,9},{9,8},{10,11... | collective-permute-start | bytes 18440 | tf_op jit(solution)/shard_map/ppermute | solution.py:417
